TPU v7x, 256 devices: a whole 4x4x8 slice. The times are simulated.
256 devices in a mesh: dp: 8 (over z), own: 32 (over x, y, core).
Axes of the slice: x: 4, y: 4, z: 8, core: 2. Of those that a mesh axis runs over, the one named last changes fastest.
Arguments:
- signals: bfloat16 [65536, 384], P(('dp', 'own')), may hold values from -6 to 6
- cotangent: bfloat16 [65536, 384], P(('dp', 'own')), may hold values from -6 to 6
- row_insertion: int32 [65536], P(('dp', 'own')), may hold values from 0 to 63, as said below
- touched: int32 [256, 4], replicated, may hold values from 0 to 63, as said below
- slot_map: int32 [64], replicated, may hold values from 0 to 63, each once
- weights: bfloat16 [64, 2, 384, 1024], P(None, None, 'own'), may hold values from -0.3125 to 0.3125
- moment1: float32 [64, 2, 384, 1024], P(None, None, 'own', 'dp'), may hold values from -25.6 to 25.6
- moment2: float32 [64, 2, 384, 1024], P(None, None, 'own', 'dp'), may hold values from 0.2048 to 6.144
Outputs:
- predicted: bfloat16 [65536, 384], P(('dp', 'own'))
- new_weights: bfloat16 [64, 2, 384, 1024], P(None, None, 'own')
- new_moment1: float32 [64, 2, 384, 1024], P(None, None, 'own', 'dp')
- new_moment2: float32 [64, 2, 384, 1024], P(None, None, 'own', 'dp')
Inputs may be any that keep to these rules, and one draw needn't show every extreme that they name: `row_insertion`: device d (dp index times the size of own plus own index) holds rows d * 256 to (d + 1) * 256 - 1; their insertions are all in row d of touched; at most 128 rows of one device name the same insertion, and on every device one insertion is named by exactly 128 rows. `touched`: each row lists 4 different insertions.
All inputs are finite; a program needn't handle non-finite values.
Results may differ from a plain program's by a relative error of at most 0.0049.
Values may be sent and summed in bfloat16 or wider, within the bound.
A program may use at most 128 MiB of HBM per device.

v0:
```python
import math

import jax
import jax.numpy as jnp
from jax import lax
from jax.sharding import PartitionSpec as P

SITES = 384
WIDTH = 1024
TOUCH = 4
CAP = 128


gelu_coef = math.sqrt(2.0 / math.pi)
cubic_coef = 0.044715
learn_rate = 0.01
highest = lax.Precision.HIGHEST


def gelu_parts(preact):
    tanh_input = gelu_coef * (preact + cubic_coef * preact * preact * preact)
    tangent = jnp.tanh(tanh_input)
    gelu_val = 0.5 * preact * (1.0 + tangent)
    slopes = 0.5 * (1.0 + tangent) + 0.5 * preact * (1.0 - tangent * tangent) * gelu_coef * (
        1.0 + 3.0 * cubic_coef * preact * preact
    )
    return (gelu_val, slopes)


def dispatch(row_ids, listed):
    match_table = (row_ids[:, None] == listed[None, :]).astype(jnp.int32)
    running = jnp.cumsum(match_table, axis=0) - 1
    slot_of = jnp.sum(match_table * jnp.arange(listed.shape[0], dtype=jnp.int32)[None, :], axis=1)
    within = jnp.sum(match_table * running, axis=1)
    return slot_of * CAP + within


def adam_step(params, moment_one, moment_two, gradient):
    moment_one = 0.9 * moment_one + 0.1 * gradient
    moment_two = 0.999 * moment_two + 0.001 * gradient * gradient
    correct_one = 1.0 - 0.9**10
    correct_two = 1.0 - 0.999**10
    updated = params - learn_rate * (moment_one / correct_one) / (
        jnp.sqrt(moment_two / correct_two) + 1e-08
    )
    return (updated.astype(jnp.bfloat16), moment_one, moment_two)


def sum_by_insertion(item_rows, arrived_grad, number):
    one_hot = (jnp.arange(number, dtype=jnp.int32)[:, None] == item_rows[None, :]).astype(
        jnp.float32
    )
    flat_grad = arrived_grad.reshape(item_rows.shape[0], -1)
    return jnp.dot(one_hot, flat_grad, precision=highest, preferred_element_type=jnp.float32)


def shards(signals, cotangent, row_insertion, touched, slot_map, weights, moment1, moment2):
    n_own = lax.axis_size("own")
    n_dp = lax.axis_size("dp")
    dp_at = lax.axis_index("dp")
    own_at = lax.axis_index("own")
    number = weights.shape[0]
    piece_rows = weights.shape[2]
    width_part = moment1.shape[3]
    stored = jnp.sum(
        jnp.where(
            touched[:, :, None] == jnp.arange(number, dtype=jnp.int32)[None, None, :],
            slot_map[None, None, :],
            0,
        ),
        axis=2,
    )
    stored_all = stored.reshape(n_dp, n_own, TOUCH)
    group_rows = lax.dynamic_index_in_dim(stored_all, dp_at, 0, keepdims=False)
    flat_rows = group_rows.reshape(-1)
    my_list = lax.dynamic_index_in_dim(touched, dp_at * n_own + own_at, 0, keepdims=False)
    places = dispatch(row_insertion, my_list)
    stacked = (
        jnp.zeros((TOUCH * CAP, 2 * SITES), signals.dtype)
        .at[places]
        .set(jnp.concatenate([signals, cotangent], axis=1))
    )
    stacked = stacked.reshape(TOUCH, CAP, 2 * SITES)
    sig_slots = stacked[:, :, :SITES]
    cot_slots = stacked[:, :, SITES:]
    read_out = None
    outgoing = jnp.take(weights, flat_rows, axis=0).reshape(n_own, TOUCH, 2, piece_rows, WIDTH)
    arrived = lax.all_to_all(outgoing, "own", split_axis=0, concat_axis=3, tiled=True)
    read_in = arrived[0, :, 0]
    read_out = arrived[0, :, 1]
    preact = jnp.einsum("kcs,ksw->kcw", sig_slots, read_in, preferred_element_type=jnp.float32)
    gelu_val, slopes = gelu_parts(preact)
    hidden = gelu_val.astype(jnp.bfloat16)
    pred_slots = jnp.einsum(
        "kcw,ksw->kcs", hidden, read_out, preferred_element_type=jnp.float32
    ).astype(jnp.bfloat16)
    back_hidden = jnp.einsum(
        "kcs,ksw->kcw", cot_slots, read_out, preferred_element_type=jnp.float32
    )
    back_pre = (back_hidden * slopes).astype(jnp.bfloat16)
    grad_in = jnp.einsum("kcs,kcw->ksw", sig_slots, back_pre, preferred_element_type=jnp.float32)
    grad_out = jnp.einsum("kcs,kcw->ksw", cot_slots, hidden, preferred_element_type=jnp.float32)
    grads = jnp.stack([grad_in, grad_out], axis=1)
    arrived_grad = lax.all_to_all(
        lax.all_to_all(grads[None, None], "dp", split_axis=5, concat_axis=0, tiled=True),
        "own",
        split_axis=4,
        concat_axis=1,
        tiled=True,
    )
    table = sum_by_insertion(stored.reshape(-1), arrived_grad, number).reshape(
        number, 2, piece_rows, width_part
    )
    own_params = lax.dynamic_slice_in_dim(weights, dp_at * width_part, width_part, 3).astype(
        jnp.float32
    )
    fresh_part, new_moment1, new_moment2 = adam_step(own_params, moment1, moment2, table)
    new_weights = lax.all_gather(fresh_part, "dp", axis=3, tiled=True)
    predicted = pred_slots.reshape(TOUCH * CAP, SITES)[places]
    return (predicted, new_weights, new_moment1, new_moment2)


def solution(mesh):
    in_specs = (
        P(("dp", "own"), None),
        P(("dp", "own"), None),
        P(("dp", "own")),
        P(),
        P(),
        P(None, None, "own", None),
        P(None, None, "own", "dp"),
        P(None, None, "own", "dp"),
    )
    out_specs = (
        P(("dp", "own"), None),
        P(None, None, "own", None),
        P(None, None, "own", "dp"),
        P(None, None, "own", "dp"),
    )
    return jax.shard_map(shards, mesh=mesh, in_specs=in_specs, out_specs=out_specs, check_vma=False)
```

profile of v0, /device:TPU:1, one launch (start us, length us, event | category | flops | bytes accessed | tf_op | source)
XLA Modules:
  0.0 813.1 jit_solution(5427315684570158318)
XLA Ops:
  7.2 1.0 select_reduce_fusion
  8.6 0.5 copy-done
  9.1 16.2 %gather_fusion = bf16[128,2,12,1024]{3,1,2,0:T(2,128)(2,1)} fusion(bf16[64,2,12,1024]{3,1,2,0:T(2,128)(2,1)S(1)} %copy-done, s32[1024]{0:T(1024)S(1)} %pad_clamp_fusion.1), kind=kCustom, calls=%fused_computation | custom fusion | bytes 12583424 | tf_op jit(solution)/shard_map/jit(_take)/gather | solution.py:87
  25.3 8.9 %broadcast_select_fusion = bf16[32,4,2,12,1024]{4,2,3,1,0:T(2,128)(2,1)} fusion(bf16[32,4,2,12,1024]{4,2,3,1,0:T(2,128)(2,1)} %bitcast.69, pred[32,4]{1,0:T(8,128)(4,1)S(1)} %copy.85), kind=kLoop, calls=%fused_computation.4 | loop fusion | flops 3145728 | bytes 12583040 | tf_op jit(solution)/shard_map/jit(_take)/select_n | solution.py:87
  34.2 8.8 %all-to-all-start = ((bf16[32,4,2,12,1024]{4,2,3,1,0:T(2,128)(2,1)}), bf16[32,4,2,12,1024]{4,2,3,1,0:T(2,128)(2,1)}, u32[]{:S(2)}, u32[]{:S(2)}) async-start(bf16[32,4,2,12,1024]{4,2,3,1,0:T(2,128)(2,1)} %broadcast_select_fusion), calls=%async_computation | async-start | bytes 12582912 | tf_op jit(solution)/shard_map/all_to_all | solution.py:88
  43.1 0.2 dynamic-slice_reduce_fusion
  43.3 1.2 reduce-window.6
  45.0 3.0 scatter_custom_fusion
  48.0 73.0 %all-to-all-done = bf16[32,4,2,12,1024]{4,2,3,1,0:T(2,128)(2,1)} async-done(((bf16[32,4,2,12,1024]{4,2,3,1,0:T(2,128)(2,1)}), bf16[32,4,2,12,1024]{4,2,3,1,0:T(2,128)(2,1)}, u32[]{:S(2)}, u32[]{:S(2)}) %all-to-all-start) | async-done | bytes 6291488 | tf_op jit(solution)/shard_map/all_to_all | solution.py:88
  121.0 6.4 copy.86
  127.4 9.8 %fusion.34 = (bf16[1,4,1,384,1024]{4,2,3,1,0:T(2,128)(2,1)S(1)}, bf16[1,4,1,384,1024]{4,2,3,1,0:T(2,128)(2,1)}) fusion(bf16[1,4,2,384,1024]{4,2,3,1,0:T(2,128)(2,1)S(1)} %bitcast.63), kind=kLoop, calls=%fused_computation.65 | loop fusion | bytes 12582912 | tf_op jit(solution)/shard_map/slice | solution.py:89
  137.2 1.2 fusion
  138.5 3.7 convolution_bitcast_fusion
  142.1 9.3 %convolution_bitcast_fusion.1 = f32[4,1,384,1024]{3,2,0,1:T(8,128)} fusion(f32[4,128,1024]{2,1,0:T(8,128)} %copy-done.1, bf16[1,4,1,384,1024]{4,2,3,1,0:T(2,128)(2,1)} %get-tuple-element.30, bf16[4,128,768]{2,1,0:T(8,128)(2,1)} %bitcast.71), kind=kOutput, calls=%fused_computation.11 | convolution fusion | flops 815267840 | bytes 12320768 | tf_op jit(solution)/shard_map/kcs,kcw->ksw/dot_general | solution.py:101
  151.4 11.9 %maximum_bitcast_fusion = f32[1,1,4,2,384,1024]{5,4,2,3,1,0:T(8,128)} fusion(f32[4,1,384,1024]{3,2,0,1:T(8,128)} %convolution_bitcast_fusion, f32[4,1,384,1024]{3,2,0,1:T(8,128)} %convolution_bitcast_fusion.1), kind=kLoop, calls=%fused_computation.3 | loop fusion | flops 3145728 | bytes 25165824 | tf_op jit(solution)/shard_map/broadcast_in_dim | solution.py:105
  163.3 14.8 %copy.94 = f32[1,1,4,2,384,1024]{4,2,3,1,0,5:T(4,128)} copy(f32[1,1,4,2,384,1024]{5,4,2,3,1,0:T(8,128)} %maximum_bitcast_fusion) | data formatting | bytes 25165824 | tf_op jit(solution)/shard_map/broadcast_in_dim | solution.py:105
  178.1 280.5 %all_to_all.51 = f32[1,1,4,2,384,1024]{4,2,3,1,0,5:T(4,128)} all-to-all(f32[1,1,4,2,384,1024]{4,2,3,1,0,5:T(4,128)} %copy.94), channel_id=1, replica_groups=mesh['dp'=8,'own'=32] {'dp'}, dimensions={5} | all-to-all | bytes 25165824 | tf_op jit(solution)/shard_map/all_to_all | solution.py:105
  458.7 14.0 %copy.95 = f32[1,1,4,2,384,8,128]{6,5,3,2,4,1,0:T(8,128)} copy(f32[1,1,4,2,384,8,128]{4,2,3,6,5,1,0:T(4,128)} %bitcast.68) | data formatting | bytes 25165824 | tf_op jit(solution)/shard_map/all_to_all | solution.py:105
  472.7 18.3 %all-to-all-start.2 = ((f32[8,1,4,2,384,128]{5,0,3,2,1,4:T(8,128)}), f32[8,1,4,2,384,128]{5,0,3,2,1,4:T(8,128)}, u32[]{:S(2)}, u32[]{:S(2)}) async-start(f32[8,1,4,2,384,128]{5,0,3,2,1,4:T(8,128)} %bitcast.66), calls=%async_computation.2 | async-start | bytes 25165824 | tf_op jit(solution)/shard_map/all_to_all | solution.py:104
  491.2 0.3 constant_dynamic-slice_fusion.1
  491.5 174.2 %all-to-all-done.2 = f32[8,1,4,2,384,128]{5,0,3,2,1,4:T(8,128)} async-done(((f32[8,1,4,2,384,128]{5,0,3,2,1,4:T(8,128)}), f32[8,1,4,2,384,128]{5,0,3,2,1,4:T(8,128)}, u32[]{:S(2)}, u32[]{:S(2)}) %all-to-all-start.2) | async-done | bytes 12582944 | tf_op jit(solution)/shard_map/all_to_all | solution.py:104
  665.7 10.0 %copy.96 = f32[8,1,4,2,384,128]{5,0,4,3,2,1:T(8,128)} copy(f32[8,1,4,2,384,128]{5,0,3,2,1,4:T(8,128)} %all-to-all-done.2) | data formatting | bytes 25165824 | tf_op jit(solution)/shard_map/all_to_all | solution.py:104
  675.6 13.0 %copy.97 = f32[8,32,1,4,2,12,128]{6,5,4,3,1,0,2:T(8,128)} copy(f32[8,32,1,4,2,12,128]{6,0,5,1,4,3,2:T(8,128)} %bitcast.64) | data formatting | bytes 25165824 | tf_op jit(solution)/shard_map/all_to_all | solution.py:104
  688.7 15.8 %reshape.122 = f32[1024,3072]{1,0:T(8,128)} reshape(f32[8,32,1,4,2,12,128]{6,5,4,3,1,0,2:T(8,128)} %copy.97) | data formatting | bytes 25165824 | tf_op jit(solution)/shard_map/reshape | solution.py:53
  704.5 12.6 %copy.98 = f32[3072,1024]{1,0:T(8,128)} copy(f32[3072,1024]{0,1:T(8,128)} %bitcast.65) | data formatting | bytes 25165824 | tf_op jit(solution)/shard_map/dot_general | solution.py:54
  717.0 11.8 %subtract_convert_fusion = (bf16[64,2,12,128]{3,0,2,1:T(8,128)(2,1)}, f32[64,2,12,128]{3,0,2,1:T(8,128)}, f32[64,2,12,128]{3,0,2,1:T(8,128)}) fusion(bf16[64,2,12,128]{3,1,2,0:T(2,128)(2,1)S(1)} %constant_dynamic-slice_fusion.1, f32[64,2,12,128]{3,1,2,0:T(2,128)} %param.14, f32[64,2,12,128]{3,1,2,0:T(2,128)} %param.15, f32[2,12,128,1024]{3,2,1,0:T(8,128)} %bitcast.67, ...), kind=kOutput, calls=%fused_computation.26 | convolution fusion | flops 2418737152 | bytes 16519168 | tf_op jit(solution)/shard_map/dot_general | solution.py:54
  728.9 4.9 convolution_convert_fusion
  733.8 1.8 gather_fusion.1
  735.7 2.7 copy.101
  738.4 1.5 copy.102
  739.8 59.6 %all-gather.2.cloned.1.call-done = bf16[64,2,12,1024]{3,0,2,1:T(8,128)(2,1)} async-done(((bf16[64,2,12,128]{3,0,2,1:T(8,128)(2,1)}), bf16[64,2,12,1024]{3,0,2,1:T(8,128)(2,1)}) %all-gather.2.cloned.1.call-update) | async-done | bytes 3145744 | tf_op jit(solution)/shard_map/all_gather | solution.py:118
  799.4 6.8 copy.100
  (35 shorter events, 1.2 us)
Async XLA Ops:
  7.2 1.9 copy-start
  34.2 8.8 %copy-start.5 = (s32[256,4]{0,1:T(4,128)S(1)}, s32[256,4]{0,1:T(4,128)}, u32[]{:S(2)}) copy-start(s32[256,4]{0,1:T(4,128)} %param.11) | copy-start | bytes 12292
  34.2 9.0 %copy-start.6 = (s32[256]{0:T(256)S(1)}, s32[256]{0:T(256)}, u32[]{:S(2)}) copy-start(s32[256]{0:T(256)} %param.10) | copy-start | bytes 3076
  34.2 10.8 %copy-start.4 = (bf16[256,384]{1,0:T(8,128)(2,1)S(1)}, bf16[256,384]{1,0:T(8,128)(2,1)}, u32[]{:S(2)}) copy-start(bf16[256,384]{1,0:T(8,128)(2,1)} %param.9) | copy-start | bytes 589828
  34.2 86.8 %all-to-all-start = ((bf16[32,4,2,12,1024]{4,2,3,1,0:T(2,128)(2,1)}), bf16[32,4,2,12,1024]{4,2,3,1,0:T(2,128)(2,1)}, u32[]{:S(2)}, u32[]{:S(2)}) async-start(bf16[32,4,2,12,1024]{4,2,3,1,0:T(2,128)(2,1)} %broadcast_select_fusion), calls=%async_computation | async-start | bytes 12582912 | tf_op jit(solution)/shard_map/all_to_all | solution.py:88
  127.4 9.8 %copy-start.2 = (bf16[512,768]{1,0:T(8,128)(2,1)S(1)}, bf16[512,768]{1,0:T(8,128)(2,1)}, u32[]{:S(2)}) copy-start(bf16[512,768]{1,0:T(8,128)(2,1)} %scatter_custom_fusion) | copy-start | bytes 2359300
  138.4 3.7 copy-start.1
  472.7 193.0 %all-to-all-start.2 = ((f32[8,1,4,2,384,128]{5,0,3,2,1,4:T(8,128)}), f32[8,1,4,2,384,128]{5,0,3,2,1,4:T(8,128)}, u32[]{:S(2)}, u32[]{:S(2)}) async-start(f32[8,1,4,2,384,128]{5,0,3,2,1,4:T(8,128)} %bitcast.66), calls=%async_computation.2 | async-start | bytes 25165824 | tf_op jit(solution)/shard_map/all_to_all | solution.py:104
  491.0 308.4 %all-gather.2.cloned.1.call-start = ((), (), s32[]{:S(2)}) async-start(), calls=%async_computation.3 | async-start | bytes 3538944 | tf_op jit(solution)/shard_map/all_gather | solution.py:118
  735.7 2.7 copy-start.3
Sparse Core Ops, SparseCore 0:
  729.0 70.3 all-gather.1
where the time goes:
time: 818 us; the launch traced here: 813 us
  waiting for transfers between devices  307 us (38%)
  blocking collectives  281 us (34%)
  local copies, waits for them, and re-layouts  127 us (16%)
  matrix products  30.9 us (4%)
  starting transfers between devices  27.2 us (3%)
  other arithmetic  26.3 us (3%)
  between operations  14.2 us (2%)
    all_to_all x1, blocking collectives, shards(): lax.all_to_all(grads[None, None], 'dp', split_axis=5, concat_axis=0, tile...  281 us
    all_to_all x1, waiting for transfers between devices, shards(): lax.all_to_all(lax.all_to_all(grads[None, None], 'dp', split_axis=5, conc...  174 us
    all_to_all x1, waiting for transfers between devices, shards(): lax.all_to_all(outgoing, 'own', split_axis=0, concat_axis=3, tiled=True)  73 us
    all_gather x1, waiting for transfers between devices, shards(): new_weights = lax.all_gather(fresh_part, 'dp', axis=3, tiled=True)  59.6 us
    all_to_all x2, local copies, waits for them, and re-layouts, shards(): lax.all_to_all(lax.all_to_all(grads[None, None], 'dp', split_axis=5, conc...  23 us
    all_to_all x1, starting transfers between devices, shards(): lax.all_to_all(lax.all_to_all(grads[None, None], 'dp', split_axis=5, conc...  18.3 us
  transfers between devices with their start and end apart: 3, of which 3 were waited for; matrix products, arithmetic and copies ran while one was open for 2% of the time, Pallas kernels for 0%

commit v1 on v0

--- a/solution.py
+++ b/solution.py
@@ -48,10 +48,10 @@
 
 def sum_by_insertion(item_rows, arrived_grad, number):
     one_hot = (jnp.arange(number, dtype=jnp.int32)[:, None] == item_rows[None, :]).astype(
-        jnp.float32
+        arrived_grad.dtype
     )
     flat_grad = arrived_grad.reshape(item_rows.shape[0], -1)
-    return jnp.dot(one_hot, flat_grad, precision=highest, preferred_element_type=jnp.float32)
+    return jnp.dot(one_hot, flat_grad, preferred_element_type=jnp.float32)
 
 
 def shards(signals, cotangent, row_insertion, touched, slot_map, weights, moment1, moment2):
@@ -100,7 +100,7 @@
     back_pre = (back_hidden * slopes).astype(jnp.bfloat16)
     grad_in = jnp.einsum("kcs,kcw->ksw", sig_slots, back_pre, preferred_element_type=jnp.float32)
     grad_out = jnp.einsum("kcs,kcw->ksw", cot_slots, hidden, preferred_element_type=jnp.float32)
-    grads = jnp.stack([grad_in, grad_out], axis=1)
+    grads = jnp.stack([grad_in, grad_out], axis=1).astype(jnp.bfloat16)
     arrived_grad = lax.all_to_all(
         lax.all_to_all(grads[None, None], "dp", split_axis=5, concat_axis=0, tiled=True),
         "own",

time: 818 us -> 531 us (0.65)
  blocking collectives: 281 us -> 146 us
  waiting for transfers between devices: 307 us -> 194 us
  local copies, waits for them, and re-layouts: 127 us -> 101 us
    all_to_all x1, blocking collectives: 281 us -> 146 us  [shards(): lax.all_to_all(grads[None, None], 'dp', split_axis=5, concat_axis=0, tile...]
    all_to_all x1, waiting for transfers between devices: 174 us -> 77.5 us  [shards(): lax.all_to_all(lax.all_to_all(grads[None, None], 'dp', split_axis=5, conc...]
    all_gather x1, waiting for transfers between devices: 59.6 us -> 43.9 us  [shards(): new_weights = lax.all_gather(fresh_part, 'dp', axis=3, tiled=True)]
    broadcast_in_dim x1 -> x0, local copies, waits for them, and re-layouts: 14.8 us -> none  [shards(): grads[None, None]]
    all_to_all x2, local copies, waits for them, and re-layouts: 23 us -> 9.51 us  [shards(): lax.all_to_all(lax.all_to_all(grads[None, None], 'dp', split_axis=5, conc...]
    broadcast_in_dim x1 -> x0, other arithmetic: 11.9 us -> none  [shards(): grads[None, None]]
    another operation x2 -> x3, local copies, waits for them, and re-layouts: 0.1 us -> 11 us  [the longest x1 10.9 us: shards(): grads = jnp.stack([grad_in, grad_out], axis=1).astype(jnp.bfloat16)]
  transfers between devices with their start and end apart: 3 -> 3, of which waited for: 3 -> 3; matrix products, arithmetic and copies ran while one was open for 2% -> 3% of each run, Pallas kernels for 0% -> 0%
where the time goes in v1:
time: 531 us; the launch traced here: 527 us
  waiting for transfers between devices  194 us (37%)
  blocking collectives  146 us (27%)
  local copies, waits for them, and re-layouts  101 us (19%)
  starting transfers between devices  26.5 us (5%)
  matrix products  24.2 us (5%)
  other arithmetic  20.5 us (4%)
  between operations  14.2 us (3%)
    all_to_all x1, blocking collectives, shards(): lax.all_to_all(grads[None, None], 'dp', split_axis=5, concat_axis=0, tile...  146 us
    all_to_all x1, waiting for transfers between devices, shards(): lax.all_to_all(lax.all_to_all(grads[None, None], 'dp', split_axis=5, conc...  77.5 us
    all_to_all x1, waiting for transfers between devices, shards(): lax.all_to_all(outgoing, 'own', split_axis=0, concat_axis=3, tiled=True)  73 us
    all_gather x1, waiting for transfers between devices, shards(): new_weights = lax.all_gather(fresh_part, 'dp', axis=3, tiled=True)  43.9 us
    all_to_all x1, starting transfers between devices, shards(): lax.all_to_all(lax.all_to_all(grads[None, None], 'dp', split_axis=5, conc...  17.7 us
    gather x1, local copies, waits for them, and re-layouts, shards(): jnp.take(weights, flat_rows, axis=0)  16.2 us
    all_to_all x1, local copies, waits for them, and re-layouts, shards(): lax.all_to_all(grads[None, None], 'dp', split_axis=5, concat_axis=0, tile...  12.3 us
    reshape x1, local copies, waits for them, and re-layouts, sum_by_insertion(): flat_grad = arrived_grad.reshape(item_rows.shape[0], -1)  12.1 us
  transfers between devices with their start and end apart: 3, of which 3 were waited for; matrix products, arithmetic and copies ran while one was open for 3% of the time, Pallas kernels for 0%

profile of v1, /device:TPU:1, one launch (start us, length us, event | category | flops | bytes accessed | tf_op | source)
XLA Modules:
  0.0 526.6 jit_solution(10570098943533189898)
XLA Ops:
  7.2 1.0 select_reduce_fusion
  8.6 0.5 copy-done
  9.1 16.2 %gather_fusion = bf16[128,2,12,1024]{3,1,2,0:T(2,128)(2,1)} fusion(bf16[64,2,12,1024]{3,1,2,0:T(2,128)(2,1)S(1)} %copy-done, s32[1024]{0:T(1024)S(1)} %pad_clamp_fusion.1), kind=kCustom, calls=%fused_computation | custom fusion | bytes 12583424 | tf_op jit(solution)/shard_map/jit(_take)/gather | solution.py:87
  25.3 8.9 %broadcast_select_fusion = bf16[32,4,2,12,1024]{4,2,3,1,0:T(2,128)(2,1)} fusion(bf16[32,4,2,12,1024]{4,2,3,1,0:T(2,128)(2,1)} %bitcast.61, pred[32,4]{1,0:T(8,128)(4,1)S(1)} %copy.85), kind=kLoop, calls=%fused_computation.3 | loop fusion | flops 3145728 | bytes 12583040 | tf_op jit(solution)/shard_map/jit(_take)/select_n | solution.py:87
  34.2 8.8 %all-to-all-start = ((bf16[32,4,2,12,1024]{4,2,3,1,0:T(2,128)(2,1)}), bf16[32,4,2,12,1024]{4,2,3,1,0:T(2,128)(2,1)}, u32[]{:S(2)}, u32[]{:S(2)}) async-start(bf16[32,4,2,12,1024]{4,2,3,1,0:T(2,128)(2,1)} %broadcast_select_fusion), calls=%async_computation | async-start | bytes 12582912 | tf_op jit(solution)/shard_map/all_to_all | solution.py:88
  43.1 0.2 dynamic-slice_reduce_fusion
  43.3 1.2 reduce-window.6
  45.0 3.0 scatter_custom_fusion
  48.0 73.0 %all-to-all-done = bf16[32,4,2,12,1024]{4,2,3,1,0:T(2,128)(2,1)} async-done(((bf16[32,4,2,12,1024]{4,2,3,1,0:T(2,128)(2,1)}), bf16[32,4,2,12,1024]{4,2,3,1,0:T(2,128)(2,1)}, u32[]{:S(2)}, u32[]{:S(2)}) %all-to-all-start) | async-done | bytes 6291488 | tf_op jit(solution)/shard_map/all_to_all | solution.py:88
  121.0 6.4 %copy.86 = bf16[1,4,2,32,12,1024]{5,2,4,3,1,0:T(2,128)(2,1)S(1)} copy(bf16[1,4,2,32,12,1024]{5,2,4,1,3,0:T(2,128)(2,1)} %bitcast.11) | data formatting | bytes 12582912 | tf_op jit(solution)/shard_map/all_to_all | solution.py:88
  127.4 9.8 %fusion.34 = (bf16[1,4,1,384,1024]{4,2,3,1,0:T(2,128)(2,1)S(1)}, bf16[1,4,1,384,1024]{4,2,3,1,0:T(2,128)(2,1)}) fusion(bf16[1,4,2,384,1024]{4,2,3,1,0:T(2,128)(2,1)S(1)} %bitcast.60), kind=kLoop, calls=%fused_computation.65 | loop fusion | bytes 12582912 | tf_op jit(solution)/shard_map/slice | solution.py:89
  137.2 1.2 fusion
  138.5 2.7 convert_bitcast_fusion
  141.2 8.3 %convert_bitcast_fusion.1 = bf16[1,1,4,1,384,1024]{5,4,2,3,1,0:T(8,128)(2,1)} fusion(f32[4,128,1024]{2,1,0:T(8,128)} %copy-done.2, bf16[1,4,1,384,1024]{4,2,3,1,0:T(2,128)(2,1)} %get-tuple-element.30, bf16[4,128,768]{2,1,0:T(8,128)(2,1)} %bitcast.68), kind=kOutput, calls=%fused_computation.9 | convolution fusion | flops 816840704 | bytes 9175040 | tf_op jit(solution)/shard_map/kcs,kcw->ksw/dot_general | solution.py:101
  149.5 6.1 %pad_maximum_fusion = bf16[1,1,4,2,384,1024]{5,4,2,3,1,0:T(8,128)(2,1)} fusion(bf16[1,1,4,1,384,1024]{5,4,2,3,1,0:T(8,128)(2,1)} %convert_bitcast_fusion, bf16[1,1,4,1,384,1024]{5,4,2,3,1,0:T(8,128)(2,1)} %convert_bitcast_fusion.1), kind=kLoop, calls=%fused_computation.4 | loop fusion | flops 3145728 | bytes 12582912 | tf_op jit(solution)/shard_map/stack | solution.py:103
  155.6 10.9 %copy.94 = bf16[1,1,4,2,384,1024]{4,2,3,1,0,5:T(4,128)(2,1)} copy(bf16[1,1,4,2,384,1024]{5,4,2,3,1,0:T(8,128)(2,1)} %pad_maximum_fusion) | data formatting | bytes 12582912 | tf_op jit(solution)/shard_map/stack | solution.py:103
  166.5 146.3 %all_to_all.51 = bf16[1,1,4,2,384,1024]{4,2,3,1,0,5:T(4,128)(2,1)} all-to-all(bf16[1,1,4,2,384,1024]{4,2,3,1,0,5:T(4,128)(2,1)} %copy.94), channel_id=1, replica_groups=mesh['dp'=8,'own'=32] {'dp'}, dimensions={5} | all-to-all | bytes 12582912 | tf_op jit(solution)/shard_map/all_to_all | solution.py:105
  312.8 12.3 %copy.95 = bf16[1,1,4,2,384,8,128]{6,5,3,2,4,1,0:T(8,128)(2,1)} copy(bf16[1,1,4,2,384,8,128]{4,2,3,6,5,1,0:T(4,128)(2,1)} %bitcast.64) | data formatting | bytes 12582912 | tf_op jit(solution)/shard_map/all_to_all | solution.py:105
  325.1 17.7 %all-to-all-start.2 = ((bf16[8,1,4,2,384,128]{5,0,3,2,1,4:T(8,128)(2,1)}), bf16[8,1,4,2,384,128]{5,0,3,2,1,4:T(8,128)(2,1)}, u32[]{:S(2)}, u32[]{:S(2)}) async-start(bf16[8,1,4,2,384,128]{5,0,3,2,1,4:T(8,128)(2,1)} %bitcast.62), calls=%async_computation.2 | async-start | bytes 12582912 | tf_op jit(solution)/shard_map/all_to_all | solution.py:104
  343.0 0.3 constant_dynamic-slice_fusion.1
  343.4 77.5 %all-to-all-done.2 = bf16[8,1,4,2,384,128]{5,0,3,2,1,4:T(8,128)(2,1)} async-done(((bf16[8,1,4,2,384,128]{5,0,3,2,1,4:T(8,128)(2,1)}), bf16[8,1,4,2,384,128]{5,0,3,2,1,4:T(8,128)(2,1)}, u32[]{:S(2)}, u32[]{:S(2)}) %all-to-all-start.2) | async-done | bytes 6291488 | tf_op jit(solution)/shard_map/all_to_all | solution.py:104
  420.8 3.9 copy.96
  424.8 5.6 %copy.97 = bf16[8,32,1,4,2,12,128]{6,5,4,3,1,0,2:T(8,128)(2,1)} copy(bf16[8,32,1,4,2,12,128]{6,0,5,1,4,3,2:T(8,128)(2,1)S(1)} %bitcast.65) | data formatting | bytes 12582912 | tf_op jit(solution)/shard_map/all_to_all | solution.py:104
  430.3 12.1 %reshape.155 = bf16[1024,3072]{1,0:T(8,128)(2,1)} reshape(bf16[8,32,1,4,2,12,128]{6,5,4,3,1,0,2:T(8,128)(2,1)} %copy.97) | data formatting | bytes 12582912 | tf_op jit(solution)/shard_map/reshape | solution.py:53
  442.4 8.7 %copy.98 = bf16[3072,1024]{1,0:T(8,128)(2,1)} copy(bf16[3072,1024]{0,1:T(8,128)(2,1)} %bitcast.66) | data formatting | bytes 12582912 | tf_op jit(solution)/shard_map/dot_general | solution.py:54
  451.1 7.0 %subtract_convert_fusion = (bf16[64,2,12,128]{3,0,2,1:T(8,128)(2,1)}, f32[64,2,12,128]{3,0,2,1:T(8,128)}, f32[64,2,12,128]{3,0,2,1:T(8,128)}) fusion(bf16[64,2,12,128]{3,1,2,0:T(2,128)(2,1)S(1)} %constant_dynamic-slice_fusion.1, f32[64,2,12,128]{3,1,2,0:T(2,128)} %param.14, f32[64,2,12,128]{3,1,2,0:T(2,128)} %param.15, ...), kind=kOutput, calls=%fused_computation.26 | convolution fusion | flops 405471232 | bytes 10227712 | tf_op jit(solution)/shard_map/dot_general | solution.py:54
  458.1 4.9 convolution_convert_fusion
  463.1 1.8 gather_fusion.1
  464.9 2.7 copy.101
  467.6 1.5 copy.102
  469.1 43.9 %all-gather.2.cloned.1.call-done = bf16[64,2,12,1024]{3,0,2,1:T(8,128)(2,1)} async-done(((bf16[64,2,12,128]{3,0,2,1:T(8,128)(2,1)}), bf16[64,2,12,1024]{3,0,2,1:T(8,128)(2,1)}) %all-gather.2.cloned.1.call-update) | async-done | bytes 3145744 | tf_op jit(solution)/shard_map/all_gather | solution.py:118
  513.0 6.8 %copy.100 = bf16[64,2,12,1024]{3,1,2,0:T(2,128)(2,1)} copy(bf16[64,2,12,1024]{3,0,2,1:T(8,128)(2,1)} %all-gather.2.cloned.1.call-done) | data formatting | bytes 6291456
  (35 shorter events, 1.2 us)
Async XLA Ops:
  7.2 1.9 copy-start
  34.2 8.8 %copy-start.5 = (s32[256,4]{0,1:T(4,128)S(1)}, s32[256,4]{0,1:T(4,128)}, u32[]{:S(2)}) copy-start(s32[256,4]{0,1:T(4,128)} %param.11) | copy-start | bytes 12292
  34.2 9.0 %copy-start.6 = (s32[256]{0:T(256)S(1)}, s32[256]{0:T(256)}, u32[]{:S(2)}) copy-start(s32[256]{0:T(256)} %param.10) | copy-start | bytes 3076
  34.2 10.8 %copy-start.4 = (bf16[256,384]{1,0:T(8,128)(2,1)S(1)}, bf16[256,384]{1,0:T(8,128)(2,1)}, u32[]{:S(2)}) copy-start(bf16[256,384]{1,0:T(8,128)(2,1)} %param.9) | copy-start | bytes 589828
  34.2 86.8 %all-to-all-start = ((bf16[32,4,2,12,1024]{4,2,3,1,0:T(2,128)(2,1)}), bf16[32,4,2,12,1024]{4,2,3,1,0:T(2,128)(2,1)}, u32[]{:S(2)}, u32[]{:S(2)}) async-start(bf16[32,4,2,12,1024]{4,2,3,1,0:T(2,128)(2,1)} %broadcast_select_fusion), calls=%async_computation | async-start | bytes 12582912 | tf_op jit(solution)/shard_map/all_to_all | solution.py:88
  127.4 9.8 %copy-start.3 = (bf16[512,768]{1,0:T(8,128)(2,1)S(1)}, bf16[512,768]{1,0:T(8,128)(2,1)}, u32[]{:S(2)}) copy-start(bf16[512,768]{1,0:T(8,128)(2,1)} %scatter_custom_fusion) | copy-start | bytes 2359300
  138.4 2.7 copy-start.2
  325.1 95.7 %all-to-all-start.2 = ((bf16[8,1,4,2,384,128]{5,0,3,2,1,4:T(8,128)(2,1)}), bf16[8,1,4,2,384,128]{5,0,3,2,1,4:T(8,128)(2,1)}, u32[]{:S(2)}, u32[]{:S(2)}) async-start(bf16[8,1,4,2,384,128]{5,0,3,2,1,4:T(8,128)(2,1)} %bitcast.62), calls=%async_computation.2 | async-start | bytes 12582912 | tf_op jit(solution)/shard_map/all_to_all | solution.py:104
  342.9 170.1 %all-gather.2.cloned.1.call-start = ((), (), s32[]{:S(2)}) async-start(), calls=%async_computation.3 | async-start | bytes 3538944 | tf_op jit(solution)/shard_map/all_gather | solution.py:118
  464.9 2.7 copy-start.1
Sparse Core Ops, SparseCore 0:
  458.2 54.6 all-gather.1

commit v2 on v1

--- a/solution.py
+++ b/solution.py
@@ -101,13 +101,11 @@
     grad_in = jnp.einsum("kcs,kcw->ksw", sig_slots, back_pre, preferred_element_type=jnp.float32)
     grad_out = jnp.einsum("kcs,kcw->ksw", cot_slots, hidden, preferred_element_type=jnp.float32)
     grads = jnp.stack([grad_in, grad_out], axis=1).astype(jnp.bfloat16)
-    arrived_grad = lax.all_to_all(
-        lax.all_to_all(grads[None, None], "dp", split_axis=5, concat_axis=0, tiled=True),
-        "own",
-        split_axis=4,
-        concat_axis=1,
-        tiled=True,
+    pieces = grads.reshape(TOUCH, 2, n_own, piece_rows, n_dp, width_part)
+    pieces = pieces.transpose(4, 2, 0, 1, 3, 5).reshape(
+        n_dp * n_own, TOUCH, 2, piece_rows, width_part
     )
+    arrived_grad = lax.all_to_all(pieces, ("dp", "own"), split_axis=0, concat_axis=0, tiled=True)
     table = sum_by_insertion(stored.reshape(-1), arrived_grad, number).reshape(
         number, 2, piece_rows, width_part
     )

time: 531 us -> 442 us (0.83)
  the two profiles are of different devices: /device:TPU:1 before, /device:TPU:32 now
where the time goes in v2:
time: 442 us; the launch traced here: 435 us
  waiting for transfers between devices  257 us (58%)
  local copies, waits for them, and re-layouts  96.1 us (22%)
  starting transfers between devices  28.2 us (6%)
  matrix products  22.6 us (5%)
  other arithmetic  17.5 us (4%)
  between operations  14.5 us (3%)
    all_to_all x1, waiting for transfers between devices, shards(): lax.all_to_all(pieces, ('dp', 'own'), split_axis=0, concat_axis=0, tiled=...  142 us
    all_to_all x1, waiting for transfers between devices, shards(): lax.all_to_all(outgoing, 'own', split_axis=0, concat_axis=3, tiled=True)  74.9 us
    all_gather x1, waiting for transfers between devices, shards(): new_weights = lax.all_gather(fresh_part, 'dp', axis=3, tiled=True)  40 us
    all_to_all x1, starting transfers between devices, shards(): lax.all_to_all(pieces, ('dp', 'own'), split_axis=0, concat_axis=0, tiled=...  20.6 us
    gather x1, local copies, waits for them, and re-layouts, shards(): jnp.take(weights, flat_rows, axis=0)  16.2 us
    unnamed x21, local copies, waits for them, and re-layouts  15.9 us
    reshape x1, local copies, waits for them, and re-layouts, sum_by_insertion(): flat_grad = arrived_grad.reshape(item_rows.shape[0], -1)  12.3 us
    reshape x1, local copies, waits for them, and re-layouts, shards(): pieces.transpose(4, 2, 0, 1, 3, 5)  10.5 us
  transfers between devices with their start and end apart: 3, of which 3 were waited for; matrix products, arithmetic and copies ran while one was open for 4% of the time, Pallas kernels for 0%

profile of v2, /device:TPU:32, one launch (start us, length us, event | category | flops | bytes accessed | tf_op | source)
XLA Modules:
  0.0 435.3 jit_solution(7643077568396394921)
XLA Ops:
  7.2 1.0 select_reduce_fusion
  8.6 0.5 copy-done
  9.1 16.2 %gather_fusion = bf16[128,2,12,1024]{3,1,2,0:T(2,128)(2,1)} fusion(bf16[64,2,12,1024]{3,1,2,0:T(2,128)(2,1)S(1)} %copy-done, s32[1024]{0:T(1024)S(1)} %pad_clamp_fusion.1), kind=kCustom, calls=%fused_computation | custom fusion | bytes 12583424 | tf_op jit(solution)/shard_map/jit(_take)/gather | solution.py:87
  25.3 8.9 %broadcast_select_fusion = bf16[32,4,2,12,1024]{4,2,3,1,0:T(2,128)(2,1)} fusion(bf16[32,4,2,12,1024]{4,2,3,1,0:T(2,128)(2,1)} %bitcast.60, pred[32,4]{1,0:T(8,128)(4,1)S(1)} %copy.89), kind=kLoop, calls=%fused_computation.3 | loop fusion | flops 3145728 | bytes 12583040 | tf_op jit(solution)/shard_map/jit(_take)/select_n | solution.py:87
  34.2 7.6 %all-to-all-start = ((bf16[32,4,2,12,1024]{4,2,3,1,0:T(2,128)(2,1)}), bf16[32,4,2,12,1024]{4,2,3,1,0:T(2,128)(2,1)}, u32[]{:S(2)}, u32[]{:S(2)}) async-start(bf16[32,4,2,12,1024]{4,2,3,1,0:T(2,128)(2,1)} %broadcast_select_fusion), calls=%async_computation | async-start | bytes 12582912 | tf_op jit(solution)/shard_map/all_to_all | solution.py:88
  42.1 1.2 reduce-window.6
  43.8 3.0 scatter_custom_fusion
  46.8 74.9 %all-to-all-done = bf16[32,4,2,12,1024]{4,2,3,1,0:T(2,128)(2,1)} async-done(((bf16[32,4,2,12,1024]{4,2,3,1,0:T(2,128)(2,1)}), bf16[32,4,2,12,1024]{4,2,3,1,0:T(2,128)(2,1)}, u32[]{:S(2)}, u32[]{:S(2)}) %all-to-all-start) | async-done | bytes 6291488 | tf_op jit(solution)/shard_map/all_to_all | solution.py:88
  121.7 6.4 %copy.90 = bf16[1,4,2,32,12,1024]{5,2,4,3,1,0:T(2,128)(2,1)S(1)} copy(bf16[1,4,2,32,12,1024]{5,2,4,1,3,0:T(2,128)(2,1)} %bitcast.11) | data formatting | bytes 12582912 | tf_op jit(solution)/shard_map/all_to_all | solution.py:88
  128.1 10.3 %fusion.40 = (bf16[1,4,1,384,1024]{4,2,3,1,0:T(2,128)(2,1)S(1)}, bf16[1,4,1,384,1024]{4,2,3,1,0:T(2,128)(2,1)}) fusion(bf16[1,4,2,384,1024]{4,2,3,1,0:T(2,128)(2,1)S(1)} %bitcast.59), kind=kLoop, calls=%fused_computation.70 | loop fusion | bytes 12582912 | tf_op jit(solution)/shard_map/slice | solution.py:89
  138.4 1.2 fusion
  139.6 1.1 convolution_convert_fusion
  140.9 0.8 copy.116
  141.7 2.9 copy.99
  144.6 8.4 %convolution_convert_fusion.1 = bf16[4,384,1024]{2,1,0:T(8,128)(2,1)} fusion(f32[4,128,1024]{2,1,0:T(8,128)} %copy-done.3, bf16[1,4,1,384,1024]{4,2,3,1,0:T(2,128)(2,1)} %get-tuple-element.30, bf16[4,128,768]{2,1,0:T(8,128)(2,1)} %bitcast.69), kind=kOutput, calls=%fused_computation.11 | convolution fusion | flops 816840704 | bytes 9175040 | tf_op jit(solution)/shard_map/kcs,kcw->ksw/dot_general | solution.py:101
  153.0 2.7 copy.115
  155.7 1.2 copy.98
  156.9 0.7 copy-done.1
  157.6 3.1 pad_maximum_fusion
  160.7 10.5 %copy.100 = bf16[256,4,2,12,128]{4,1,3,2,0:T(4,128)(2,1)} copy(bf16[256,4,2,12,128]{4,0,3,2,1:T(8,128)(2,1)} %bitcast.62) | data formatting | bytes 12582912 | tf_op jit(solution)/shard_map/reshape | solution.py:105
  171.2 20.6 %all-to-all-start.1 = ((bf16[256,4,2,12,128]{4,1,3,2,0:T(4,128)(2,1)}), bf16[256,4,2,12,128]{4,1,3,2,0:T(4,128)(2,1)}, u32[]{:S(2)}, u32[]{:S(2)}) async-start(bf16[256,4,2,12,128]{4,1,3,2,0:T(4,128)(2,1)} %copy.100), calls=%async_computation.1 | async-start | bytes 12582912 | tf_op jit(solution)/shard_map/all_to_all | solution.py:108
  192.2 141.6 %all-to-all-done.1 = bf16[256,4,2,12,128]{4,1,3,2,0:T(4,128)(2,1)} async-done(((bf16[256,4,2,12,128]{4,1,3,2,0:T(4,128)(2,1)}), bf16[256,4,2,12,128]{4,1,3,2,0:T(4,128)(2,1)}, u32[]{:S(2)}, u32[]{:S(2)}) %all-to-all-start.1) | async-done | bytes 6291488 | tf_op jit(solution)/shard_map/all_to_all | solution.py:108
  333.9 8.7 %copy.101 = bf16[256,4,2,12,128]{4,3,2,1,0:T(8,128)(2,1)} copy(bf16[256,4,2,12,128]{4,1,3,2,0:T(4,128)(2,1)} %all-to-all-done.1) | data formatting | bytes 12582912 | tf_op jit(solution)/shard_map/all_to_all | solution.py:108
  342.5 12.3 %reshape.132 = bf16[1024,3072]{1,0:T(8,128)(2,1)} reshape(bf16[256,4,2,12,128]{4,3,2,1,0:T(8,128)(2,1)} %copy.101) | data formatting | bytes 12582912 | tf_op jit(solution)/shard_map/reshape | solution.py:53
  354.8 8.7 %copy.102 = bf16[3072,1024]{1,0:T(8,128)(2,1)} copy(bf16[3072,1024]{0,1:T(8,128)(2,1)} %bitcast.63) | data formatting | bytes 12582912 | tf_op jit(solution)/shard_map/dot_general | solution.py:54
  363.4 7.0 %subtract_convert_fusion = (bf16[64,2,12,128]{3,0,2,1:T(8,128)(2,1)}, f32[64,2,12,128]{3,0,2,1:T(8,128)}, f32[64,2,12,128]{3,0,2,1:T(8,128)}) fusion(bf16[64,2,12,128]{3,1,2,0:T(2,128)(2,1)S(1)} %constant_dynamic-slice_fusion.1, f32[64,2,12,128]{3,1,2,0:T(2,128)} %param.14, f32[64,2,12,128]{3,1,2,0:T(2,128)} %param.15, ...), kind=kOutput, calls=%fused_computation.31 | convolution fusion | flops 405471232 | bytes 10227712 | tf_op jit(solution)/shard_map/dot_general | solution.py:54
  370.5 4.9 %convolution_convert_fusion.2 = bf16[4,128,384]{2,1,0:T(8,128)(2,1)S(1)} fusion(bf16[1,4,1,384,1024]{4,2,3,1,0:T(2,128)(2,1)} %get-tuple-element.30, f32[4,128,1024]{2,1,0:T(8,128)} %copy-done.3), kind=kOutput, calls=%fused_computation.20 | convolution fusion | flops 407568384 | bytes 5636096 | tf_op jit(solution)/shard_map/kcw,ksw->kcs/dot_general | solution.py:94
  375.4 1.8 gather_fusion.1
  377.2 2.7 copy.105
  380.0 1.5 copy.106
  381.4 40.0 %all-gather.2.cloned.1.call-done = bf16[64,2,12,1024]{3,0,2,1:T(8,128)(2,1)} async-done(((bf16[64,2,12,128]{3,0,2,1:T(8,128)(2,1)}), bf16[64,2,12,1024]{3,0,2,1:T(8,128)(2,1)}) %all-gather.2.cloned.1.call-update) | async-done | bytes 3145744 | tf_op jit(solution)/shard_map/all_gather | solution.py:116
  421.4 6.8 %copy.104 = bf16[64,2,12,1024]{3,1,2,0:T(2,128)(2,1)} copy(bf16[64,2,12,1024]{3,0,2,1:T(8,128)(2,1)} %all-gather.2.cloned.1.call-done) | data formatting | bytes 6291456
  (38 shorter events, 2.0 us)
Async XLA Ops:
  7.2 1.9 copy-start
  34.2 7.6 %copy-start.6 = (s32[256,4]{0,1:T(4,128)S(1)}, s32[256,4]{0,1:T(4,128)}, u32[]{:S(2)}) copy-start(s32[256,4]{0,1:T(4,128)} %param.11) | copy-start | bytes 12292
  34.2 7.8 %copy-start.7 = (s32[256]{0:T(256)S(1)}, s32[256]{0:T(256)}, u32[]{:S(2)}) copy-start(s32[256]{0:T(256)} %param.10) | copy-start | bytes 3076
  34.2 9.6 %copy-start.5 = (bf16[256,384]{1,0:T(8,128)(2,1)S(1)}, bf16[256,384]{1,0:T(8,128)(2,1)}, u32[]{:S(2)}) copy-start(bf16[256,384]{1,0:T(8,128)(2,1)} %param.9) | copy-start | bytes 589828
  34.2 87.4 %all-to-all-start = ((bf16[32,4,2,12,1024]{4,2,3,1,0:T(2,128)(2,1)}), bf16[32,4,2,12,1024]{4,2,3,1,0:T(2,128)(2,1)}, u32[]{:S(2)}, u32[]{:S(2)}) async-start(bf16[32,4,2,12,1024]{4,2,3,1,0:T(2,128)(2,1)} %broadcast_select_fusion), calls=%async_computation | async-start | bytes 12582912 | tf_op jit(solution)/shard_map/all_to_all | solution.py:88
  128.1 10.3 %copy-start.4 = (bf16[512,768]{1,0:T(8,128)(2,1)S(1)}, bf16[512,768]{1,0:T(8,128)(2,1)}, u32[]{:S(2)}) copy-start(bf16[512,768]{1,0:T(8,128)(2,1)} %scatter_custom_fusion) | copy-start | bytes 2359300
  139.6 1.3 copy-start.3
  155.7 1.9 copy-start.1
  171.2 162.7 %all-to-all-start.1 = ((bf16[256,4,2,12,128]{4,1,3,2,0:T(4,128)(2,1)}), bf16[256,4,2,12,128]{4,1,3,2,0:T(4,128)(2,1)}, u32[]{:S(2)}, u32[]{:S(2)}) async-start(bf16[256,4,2,12,128]{4,1,3,2,0:T(4,128)(2,1)} %copy.100), calls=%async_computation.1 | async-start | bytes 12582912 | tf_op jit(solution)/shard_map/all_to_all | solution.py:108
  191.7 229.7 %all-gather.2.cloned.1.call-start = ((), (), s32[]{:S(2)}) async-start(), calls=%async_computation.2 | async-start | bytes 3538944 | tf_op jit(solution)/shard_map/all_gather | solution.py:116
  377.2 2.7 copy-start.2
Sparse Core Ops, SparseCore 0:
  370.6 50.8 all-gather.1

commit v3 on v2

--- a/solution.py
+++ b/solution.py
@@ -1,14 +1,89 @@
+import functools
 import math
 
 import jax
 import jax.numpy as jnp
 from jax import lax
+from jax.experimental import pallas as pl
+from jax.experimental.pallas import tpu as pltpu
 from jax.sharding import PartitionSpec as P
 
 SITES = 384
 WIDTH = 1024
 TOUCH = 4
 CAP = 128
+
+MESH = pl.DeviceIdType.MESH
+
+def _a2a_kernel(n_dp, n_own, full, x_ref, o_ref, send_sems, recv_sems, local_sem):
+    dp_at = lax.axis_index("dp")
+    own_at = lax.axis_index("own")
+    if full:
+        n = n_dp * n_own
+        me = dp_at * n_own + own_at
+        def dev(k):
+            return (k // n_own, k % n_own)
+    else:
+        n = n_own
+        me = own_at
+        def dev(k):
+            return (dp_at, k)
+    barrier = pltpu.get_barrier_semaphore()
+
+    def greet(i, c):
+        peer = lax.rem(me + i, n)
+        pl.semaphore_signal(barrier, 1, device_id=dev(peer), device_id_type=MESH)
+        return c
+
+    lax.fori_loop(1, n, greet, 0)
+    pl.semaphore_wait(barrier, n - 1)
+    local = pltpu.make_async_copy(x_ref.at[me], o_ref.at[me], local_sem)
+    local.start()
+
+    def send(i, c):
+        peer = lax.rem(me + i, n)
+        pltpu.make_async_remote_copy(
+            src_ref=x_ref.at[peer], dst_ref=o_ref.at[me],
+            send_sem=send_sems.at[peer], recv_sem=recv_sems.at[me],
+            device_id=dev(peer), device_id_type=MESH,
+        ).start()
+        return c
+
+    lax.fori_loop(1, n, send, 0)
+
+    def finish(i, c):
+        peer = lax.rem(me + i, n)
+        src = lax.rem(me + n - i, n)
+        pltpu.make_async_remote_copy(
+            src_ref=x_ref.at[peer], dst_ref=o_ref.at[src],
+            send_sem=send_sems.at[peer], recv_sem=recv_sems.at[src],
+            device_id=dev(peer), device_id_type=MESH,
+        ).wait_send()
+        pltpu.make_async_remote_copy(
+            src_ref=x_ref.at[peer], dst_ref=o_ref.at[src],
+            send_sem=send_sems.at[peer], recv_sem=recv_sems.at[src],
+            device_id=dev(src), device_id_type=MESH,
+        ).wait_recv()
+        return c
+
+    lax.fori_loop(1, n, finish, 0)
+    local.wait()
+
+
+def exchange(x, n_dp, n_own, full, cid):
+    n = x.shape[0]
+    return pl.pallas_call(
+        functools.partial(_a2a_kernel, n_dp, n_own, full),
+        out_shape=jax.ShapeDtypeStruct(x.shape, x.dtype),
+        in_specs=[pl.BlockSpec(memory_space=pl.ANY)],
+        out_specs=pl.BlockSpec(memory_space=pl.ANY),
+        scratch_shapes=[
+            pltpu.SemaphoreType.DMA((n,)),
+            pltpu.SemaphoreType.DMA((n,)),
+            pltpu.SemaphoreType.DMA,
+        ],
+        compiler_params=pltpu.CompilerParams(collective_id=cid, has_side_effects=True),
+    )(x)
 
 
 gelu_coef = math.sqrt(2.0 / math.pi)
@@ -105,7 +180,9 @@
     pieces = pieces.transpose(4, 2, 0, 1, 3, 5).reshape(
         n_dp * n_own, TOUCH, 2, piece_rows, width_part
     )
-    arrived_grad = lax.all_to_all(pieces, ("dp", "own"), split_axis=0, concat_axis=0, tiled=True)
+    arrived_grad = exchange(
+        pieces.reshape(n_dp * n_own, TOUCH * 2 * piece_rows, width_part), n_dp, n_own, True, 0
+    )
     table = sum_by_insertion(stored.reshape(-1), arrived_grad, number).reshape(
         number, 2, piece_rows, width_part
     )

time: 442 us -> 467 us (1.057)
  the two profiles are of different devices: /device:TPU:32 before, /device:TPU:1 now
where the time goes in v3:
time: 467 us; the launch traced here: 463 us
  Pallas kernels  182 us (39%)
  waiting for transfers between devices  141 us (30%)
  local copies, waits for them, and re-layouts  80.3 us (17%)
  matrix products  21.1 us (5%)
  other arithmetic  15 us (3%)
  between operations  14.2 us (3%)
  starting transfers between devices  8.82 us (2%)
    pallas_call x1, Pallas kernels, exchange(): pl.pallas_call(functools.partial(_a2a_kernel, n_dp, n_own, full), out_sha...  182 us
    all_to_all x1, waiting for transfers between devices, shards(): lax.all_to_all(outgoing, 'own', split_axis=0, concat_axis=3, tiled=True)  72.5 us
    all_gather x1, waiting for transfers between devices, shards(): new_weights = lax.all_gather(fresh_part, 'dp', axis=3, tiled=True)  68.5 us
    gather x1, local copies, waits for them, and re-layouts, shards(): jnp.take(weights, flat_rows, axis=0)  16.2 us
    unnamed x27, local copies, waits for them, and re-layouts  14.7 us
    reshape x1, local copies, waits for them, and re-layouts, sum_by_insertion(): flat_grad = arrived_grad.reshape(item_rows.shape[0], -1)  10.3 us
    slice x1, local copies, waits for them, and re-layouts, shards(): read_in = arrived[0, :, 0]  9.85 us
  transfers between devices with their start and end apart: 2, of which 2 were waited for; matrix products, arithmetic and copies ran while one was open for 3% of the time, Pallas kernels for 0%

profile of v3, /device:TPU:1, one launch (start us, length us, event | category | flops | bytes accessed | tf_op | source)
XLA Modules:
  0.0 462.8 jit_solution(3832383058106328868)
XLA Ops:
  7.2 1.0 select_reduce_fusion
  8.6 0.5 copy-done
  9.1 16.2 %gather_fusion = bf16[128,2,12,1024]{3,1,2,0:T(2,128)(2,1)} fusion(bf16[64,2,12,1024]{3,1,2,0:T(2,128)(2,1)S(1)} %copy-done, s32[1024]{0:T(1024)S(1)} %pad_clamp_fusion.1), kind=kCustom, calls=%fused_computation | custom fusion | bytes 12583424 | tf_op jit(solution)/shard_map/jit(_take)/gather | solution.py:162
  25.3 8.9 %broadcast_select_fusion = bf16[32,4,2,12,1024]{4,2,3,1,0:T(2,128)(2,1)} fusion(bf16[32,4,2,12,1024]{4,2,3,1,0:T(2,128)(2,1)} %bitcast.60, pred[32,4]{1,0:T(8,128)(4,1)S(1)} %copy.71), kind=kLoop, calls=%fused_computation.3 | loop fusion | flops 3145728 | bytes 12583040 | tf_op jit(solution)/shard_map/jit(_take)/select_n | solution.py:162
  34.2 8.8 %all-to-all-start = ((bf16[32,4,2,12,1024]{4,2,3,1,0:T(2,128)(2,1)}), bf16[32,4,2,12,1024]{4,2,3,1,0:T(2,128)(2,1)}, u32[]{:S(2)}, u32[]{:S(2)}) async-start(bf16[32,4,2,12,1024]{4,2,3,1,0:T(2,128)(2,1)} %broadcast_select_fusion), calls=%async_computation | async-start | bytes 12582912 | tf_op jit(solution)/shard_map/all_to_all | solution.py:163
  43.5 1.2 reduce-window.6
  45.2 3.0 scatter_custom_fusion
  48.2 0.3 constant_dynamic-slice_fusion.1
  48.5 72.5 %all-to-all-done = bf16[32,4,2,12,1024]{4,2,3,1,0:T(2,128)(2,1)} async-done(((bf16[32,4,2,12,1024]{4,2,3,1,0:T(2,128)(2,1)}), bf16[32,4,2,12,1024]{4,2,3,1,0:T(2,128)(2,1)}, u32[]{:S(2)}, u32[]{:S(2)}) %all-to-all-start) | async-done | bytes 6291488 | tf_op jit(solution)/shard_map/all_to_all | solution.py:163
  121.0 6.4 %copy.72 = bf16[1,4,2,32,12,1024]{5,2,4,3,1,0:T(2,128)(2,1)S(1)} copy(bf16[1,4,2,32,12,1024]{5,2,4,1,3,0:T(2,128)(2,1)} %bitcast.11) | data formatting | bytes 12582912 | tf_op jit(solution)/shard_map/all_to_all | solution.py:163
  127.4 9.8 %fusion.40 = (bf16[1,4,1,384,1024]{4,2,3,1,0:T(2,128)(2,1)S(1)}, bf16[1,4,1,384,1024]{4,2,3,1,0:T(2,128)(2,1)}) fusion(bf16[1,4,2,384,1024]{4,2,3,1,0:T(2,128)(2,1)S(1)} %bitcast.59), kind=kLoop, calls=%fused_computation.70 | loop fusion | bytes 12582912 | tf_op jit(solution)/shard_map/slice | solution.py:164
  137.3 1.2 fusion
  138.5 1.1 convolution_convert_fusion
  139.5 0.2 copy-done.3
  139.8 0.8 copy.97
  140.6 2.9 copy.81
  143.5 8.4 %convolution_convert_fusion.1 = bf16[4,384,1024]{2,1,0:T(8,128)(2,1)} fusion(f32[4,128,1024]{2,1,0:T(8,128)} %copy-done.3, bf16[1,4,1,384,1024]{4,2,3,1,0:T(2,128)(2,1)} %get-tuple-element.26, bf16[4,128,768]{2,1,0:T(8,128)(2,1)} %bitcast.69), kind=kOutput, calls=%fused_computation.11 | convolution fusion | flops 816840704 | bytes 9175040 | tf_op jit(solution)/shard_map/kcs,kcw->ksw/dot_general | solution.py:176
  151.9 2.7 copy.96
  154.6 1.2 copy.80
  155.8 0.7 copy-done.2
  156.5 0.6 pad_maximum_fusion
  157.1 6.9 %copy.82.x_ref = bf16[256,96,128]{2,1,0:T(8,128)(2,1)} copy(bf16[256,96,128]{2,0,1:T(8,128)(2,1)S(1)} %bitcast.62) | data formatting | bytes 12582912 | tf_op jit(solution)/shard_map/reshape;reshape | solution.py:184
  163.9 182.3 %shard_map.111 = bf16[256,96,128]{2,1,0:T(8,128)(2,1)} custom-call(bf16[256,96,128]{2,1,0:T(8,128)(2,1)} %copy.82.x_ref), custom_call_target="tpu_custom_call" | custom-call | tf_op jit(solution)/shard_map/pallas_call | solution.py:75
  346.3 10.3 %reshape.128 = bf16[1024,3072]{1,0:T(8,128)(2,1)} reshape(bf16[256,96,128]{2,1,0:T(8,128)(2,1)} %shard_map.111) | data formatting | bytes 12582912 | tf_op jit(solution)/shard_map/reshape | solution.py:128
  356.6 8.7 %copy.83 = bf16[3072,1024]{1,0:T(8,128)(2,1)} copy(bf16[3072,1024]{0,1:T(8,128)(2,1)} %bitcast.63) | data formatting | bytes 12582912 | tf_op jit(solution)/shard_map/dot_general | solution.py:129
  365.4 6.1 %subtract_convert_fusion = (bf16[64,2,12,128]{3,0,2,1:T(8,128)(2,1)}, f32[64,2,12,128]{3,0,2,1:T(8,128)S(1)}, f32[64,2,12,128]{3,0,2,1:T(8,128)S(1)}) fusion(bf16[64,2,12,128]{3,1,2,0:T(2,128)(2,1)S(1)} %constant_dynamic-slice_fusion.1, f32[64,2,12,128]{3,1,2,0:T(2,128)S(1)} %copy-done.6, f32[64,2,12,128]{3,1,2,0:T(2,128)S(1)} %copy-done.7, ...), kind=kOutput, calls=%fused_computation.31 | convolution fusion | flops 405471232 | bytes 10227712 | tf_op jit(solution)/shard_map/dot_general | solution.py:129
  371.5 1.5 copy.86
  373.0 1.5 copy.87
  374.5 4.3 convolution_convert_fusion.2
  378.8 1.8 gather_fusion.1
  380.6 68.5 %all-gather.2.cloned.1.call-done = bf16[64,2,12,1024]{3,0,2,1:T(8,128)(2,1)} async-done(((bf16[64,2,12,128]{3,0,2,1:T(8,128)(2,1)}), bf16[64,2,12,1024]{3,0,2,1:T(8,128)(2,1)}) %all-gather.2.cloned.1.call-update) | async-done | bytes 3145744 | tf_op jit(solution)/shard_map/all_gather | solution.py:193
  449.1 6.8 %copy.85 = bf16[64,2,12,1024]{3,1,2,0:T(2,128)(2,1)} copy(bf16[64,2,12,1024]{3,0,2,1:T(8,128)(2,1)} %all-gather.2.cloned.1.call-done) | data formatting | bytes 6291456
  (42 shorter events, 1.4 us)
Async XLA Ops:
  7.2 1.9 copy-start
  34.2 9.0 %copy-start.9 = (s32[256,4]{0,1:T(4,128)S(1)}, s32[256,4]{0,1:T(4,128)}, u32[]{:S(2)}) copy-start(s32[256,4]{0,1:T(4,128)} %param.11) | copy-start | bytes 12292
  34.2 9.2 %copy-start.10 = (s32[256]{0:T(256)S(1)}, s32[256]{0:T(256)}, u32[]{:S(2)}) copy-start(s32[256]{0:T(256)} %param.10) | copy-start | bytes 3076
  34.2 10.9 %copy-start.8 = (bf16[256,384]{1,0:T(8,128)(2,1)S(1)}, bf16[256,384]{1,0:T(8,128)(2,1)}, u32[]{:S(2)}) copy-start(bf16[256,384]{1,0:T(8,128)(2,1)} %param.9) | copy-start | bytes 589828
  34.2 86.8 %all-to-all-start = ((bf16[32,4,2,12,1024]{4,2,3,1,0:T(2,128)(2,1)}), bf16[32,4,2,12,1024]{4,2,3,1,0:T(2,128)(2,1)}, u32[]{:S(2)}, u32[]{:S(2)}) async-start(bf16[32,4,2,12,1024]{4,2,3,1,0:T(2,128)(2,1)} %broadcast_select_fusion), calls=%async_computation | async-start | bytes 12582912 | tf_op jit(solution)/shard_map/all_to_all | solution.py:163
  43.0 406.1 %all-gather.2.cloned.1.call-start = ((), (), s32[]{:S(2)}) async-start(), calls=%async_computation.1 | async-start | bytes 3538944 | tf_op jit(solution)/shard_map/all_gather | solution.py:193
  127.4 9.9 %copy-start.5 = (bf16[512,768]{1,0:T(8,128)(2,1)S(1)}, bf16[512,768]{1,0:T(8,128)(2,1)}, u32[]{:S(2)}) copy-start(bf16[512,768]{1,0:T(8,128)(2,1)} %scatter_custom_fusion) | copy-start | bytes 2359300
  138.5 1.3 copy-start.3
  154.6 1.9 copy-start.2
  356.6 8.8 %copy-start.6 = (f32[64,2,12,128]{3,1,2,0:T(2,128)S(1)}, f32[64,2,12,128]{3,1,2,0:T(2,128)}, u32[]{:S(2)}) copy-start(f32[64,2,12,128]{3,1,2,0:T(2,128)} %param.14) | copy-start | bytes 2359300
  356.6 8.8 %copy-start.7 = (f32[64,2,12,128]{3,1,2,0:T(2,128)S(1)}, f32[64,2,12,128]{3,1,2,0:T(2,128)}, u32[]{:S(2)}) copy-start(f32[64,2,12,128]{3,1,2,0:T(2,128)} %param.15) | copy-start | bytes 2359300
  371.5 3.0 copy-start.4
  378.8 77.1 %copy-start.1 = (bf16[64,2,12,1024]{3,1,2,0:T(2,128)(2,1)S(1)}, bf16[64,2,12,1024]{3,1,2,0:T(2,128)(2,1)}, u32[]{:S(2)}) copy-start(bf16[64,2,12,1024]{3,1,2,0:T(2,128)(2,1)} %param.13) | copy-start | bytes 9437188
Sparse Core Ops, SparseCore 0:
  371.6 77.4 all-gather.1

commit v4 on v3

--- a/solution.py
+++ b/solution.py
@@ -137,6 +137,7 @@
     number = weights.shape[0]
     piece_rows = weights.shape[2]
     width_part = moment1.shape[3]
+    pairs = n_dp * TOUCH
     stored = jnp.sum(
         jnp.where(
             touched[:, :, None] == jnp.arange(number, dtype=jnp.int32)[None, None, :],
@@ -145,9 +146,7 @@
         ),
         axis=2,
     )
-    stored_all = stored.reshape(n_dp, n_own, TOUCH)
-    group_rows = lax.dynamic_index_in_dim(stored_all, dp_at, 0, keepdims=False)
-    flat_rows = group_rows.reshape(-1)
+    peer_rows = stored.reshape(n_dp, n_own, TOUCH).transpose(1, 0, 2).reshape(-1)
     my_list = lax.dynamic_index_in_dim(touched, dp_at * n_own + own_at, 0, keepdims=False)
     places = dispatch(row_insertion, my_list)
     stacked = (
@@ -155,40 +154,37 @@
         .at[places]
         .set(jnp.concatenate([signals, cotangent], axis=1))
     )
-    stacked = stacked.reshape(TOUCH, CAP, 2 * SITES)
+    stacked = lax.all_gather(stacked.reshape(TOUCH, CAP, 2 * SITES), "dp", axis=0, tiled=True)
+    stacked = stacked.reshape(pairs, CAP, 2 * SITES)
     sig_slots = stacked[:, :, :SITES]
     cot_slots = stacked[:, :, SITES:]
-    read_out = None
-    outgoing = jnp.take(weights, flat_rows, axis=0).reshape(n_own, TOUCH, 2, piece_rows, WIDTH)
-    arrived = lax.all_to_all(outgoing, "own", split_axis=0, concat_axis=3, tiled=True)
-    read_in = arrived[0, :, 0]
-    read_out = arrived[0, :, 1]
+    my_width = lax.dynamic_slice_in_dim(weights, dp_at * width_part, width_part, 3)
+    outgoing = jnp.take(my_width, peer_rows, axis=0).reshape(
+        n_own, pairs, 2, piece_rows, width_part
+    )
+    arrived = lax.all_to_all(outgoing, "own", split_axis=0, concat_axis=0, tiled=True)
+    arrived = arrived.transpose(1, 2, 0, 3, 4).reshape(pairs, 2, SITES, width_part)
+    read_in = arrived[:, 0]
+    read_out = arrived[:, 1]
     preact = jnp.einsum("kcs,ksw->kcw", sig_slots, read_in, preferred_element_type=jnp.float32)
     gelu_val, slopes = gelu_parts(preact)
     hidden = gelu_val.astype(jnp.bfloat16)
-    pred_slots = jnp.einsum(
-        "kcw,ksw->kcs", hidden, read_out, preferred_element_type=jnp.float32
-    ).astype(jnp.bfloat16)
+    pred_part = jnp.einsum("kcw,ksw->kcs", hidden, read_out, preferred_element_type=jnp.float32)
     back_hidden = jnp.einsum(
         "kcs,ksw->kcw", cot_slots, read_out, preferred_element_type=jnp.float32
     )
     back_pre = (back_hidden * slopes).astype(jnp.bfloat16)
     grad_in = jnp.einsum("kcs,kcw->ksw", sig_slots, back_pre, preferred_element_type=jnp.float32)
     grad_out = jnp.einsum("kcs,kcw->ksw", cot_slots, hidden, preferred_element_type=jnp.float32)
+    pred_slots = lax.psum_scatter(pred_part, "dp", scatter_dimension=0, tiled=True)
+    pred_slots = pred_slots.astype(jnp.bfloat16)
     grads = jnp.stack([grad_in, grad_out], axis=1).astype(jnp.bfloat16)
-    pieces = grads.reshape(TOUCH, 2, n_own, piece_rows, n_dp, width_part)
-    pieces = pieces.transpose(4, 2, 0, 1, 3, 5).reshape(
-        n_dp * n_own, TOUCH, 2, piece_rows, width_part
-    )
-    arrived_grad = exchange(
-        pieces.reshape(n_dp * n_own, TOUCH * 2 * piece_rows, width_part), n_dp, n_own, True, 0
-    )
-    table = sum_by_insertion(stored.reshape(-1), arrived_grad, number).reshape(
+    pieces = grads.reshape(pairs, 2, n_own, piece_rows, width_part).transpose(2, 0, 1, 3, 4)
+    arrived_grad = lax.all_to_all(pieces, "own", split_axis=0, concat_axis=0, tiled=True)
+    table = sum_by_insertion(peer_rows, arrived_grad, number).reshape(
         number, 2, piece_rows, width_part
     )
-    own_params = lax.dynamic_slice_in_dim(weights, dp_at * width_part, width_part, 3).astype(
-        jnp.float32
-    )
+    own_params = my_width.astype(jnp.float32)
     fresh_part, new_moment1, new_moment2 = adam_step(own_params, moment1, moment2, table)
     new_weights = lax.all_gather(fresh_part, "dp", axis=3, tiled=True)
     predicted = pred_slots.reshape(TOUCH * CAP, SITES)[places]

time: 467 us -> 428 us (0.916)
  Pallas kernels: 182 us -> 0 us
  blocking collectives: 0 us -> 81.5 us
  waiting for transfers between devices: 141 us -> 197 us
  matrix products: 21.1 us -> 32.2 us
    pallas_call x1 -> x0, Pallas kernels: 182 us -> none  [exchange(): pl.pallas_call(functools.partial(_a2a_kernel, n_dp, n_own, full), out_sha...]
    all_to_all x0 -> x1, blocking collectives: none -> 81.5 us  [shards(): lax.all_to_all(outgoing, 'own', split_axis=0, concat_axis=0, tiled=True)]
    reduce_scatter x0 -> x1, waiting for transfers between devices: none -> 72.5 us  [shards(): lax.psum_scatter(pred_part, 'dp', scatter_dimension=0, tiled=True)]
    all_gather x1, waiting for transfers between devices: 68.5 us -> 46.7 us  [shards(): new_weights = lax.all_gather(fresh_part, 'dp', axis=3, tiled=True)]
    slice x3, local copies, waits for them, and re-layouts: 10 us -> 2.92 us  [the longest x1 2.74 us: shards(): read_in = arrived[:, 0]]
    select_n x2, other arithmetic: 8.94 us -> 3.75 us  [shards(): jnp.take(my_width, peer_rows, axis=0)]
    all_to_all x1, waiting for transfers between devices: 72.5 us -> 77.7 us  [shards(): lax.all_to_all(pieces, 'own', split_axis=0, concat_axis=0, tiled=True)]
    another operation x5 -> x4, local copies, waits for them, and re-layouts: 11.1 us -> 6.04 us  [the longest x1 6.88 us: shards(): pieces.reshape(n_dp * n_own, TOUCH * 2 * piece_rows, width_part)]
  transfers between devices with their start and end apart: 2 -> 4, of which waited for: 2 -> 3; matrix products, arithmetic and copies ran while one was open for 3% -> 11% of each run, Pallas kernels for 0% -> 0%
where the time goes in v4:
time: 428 us; the launch traced here: 423 us
  waiting for transfers between devices  197 us (46%)
  blocking collectives  81.5 us (19%)
  local copies, waits for them, and re-layouts  81 us (19%)
  matrix products  32.2 us (8%)
  between operations  14.1 us (3%)
  other arithmetic  12.2 us (3%)
  starting transfers between devices  4.95 us (1%)
    all_to_all x1, blocking collectives, shards(): lax.all_to_all(outgoing, 'own', split_axis=0, concat_axis=0, tiled=True)  81.5 us
    all_to_all x1, waiting for transfers between devices, shards(): lax.all_to_all(pieces, 'own', split_axis=0, concat_axis=0, tiled=True)  77.7 us
    reduce_scatter x1, waiting for transfers between devices, shards(): lax.psum_scatter(pred_part, 'dp', scatter_dimension=0, tiled=True)  72.5 us
    all_gather x1, waiting for transfers between devices, shards(): new_weights = lax.all_gather(fresh_part, 'dp', axis=3, tiled=True)  46.7 us
    gather x1, local copies, waits for them, and re-layouts, shards(): jnp.take(my_width, peer_rows, axis=0)  20.7 us
    unnamed x19, local copies, waits for them, and re-layouts  12.6 us
    reshape x1, local copies, waits for them, and re-layouts, sum_by_insertion(): flat_grad = arrived_grad.reshape(item_rows.shape[0], -1)  12.2 us
    dot_general x1, matrix products, shards(): jnp.einsum('kcs,kcw->ksw', sig_slots, back_pre, preferred_element_type=jn...  11.4 us
  transfers between devices with their start and end apart: 4, of which 3 were waited for; matrix products, arithmetic and copies ran while one was open for 11% of the time, Pallas kernels for 0%

profile of v4, /device:TPU:1, one launch (start us, length us, event | category | flops | bytes accessed | tf_op | source)
XLA Modules:
  0.0 422.9 jit_solution(2358769315195918064)
XLA Ops:
  7.2 1.0 dynamic-slice_reduce_fusion
  8.3 0.8 compare_convert_fusion
  9.0 1.2 reduce-window.6
  10.6 0.8 fusion.43
  11.4 3.1 scatter_custom_fusion
  14.5 0.8 select_reduce_fusion
  16.5 20.7 %gather_fusion = bf16[1024,2,12,128]{3,1,2,0:T(2,128)(2,1)} fusion(bf16[64,2,12,128]{3,1,2,0:T(2,128)(2,1)S(1)} %constant_dynamic-slice_fusion, s32[1024]{0:T(1024)S(1)} %broadcast_clamp_fusion), kind=kCustom, calls=%fused_computation | custom fusion | bytes 12587008 | tf_op jit(solution)/shard_map/jit(_take)/gather | solution.py:162
  37.2 3.7 copy_select_fusion
  40.9 81.5 %all_to_all.10 = bf16[32,32,2,12,128]{4,1,3,2,0:T(8,128)(2,1)S(1)} all-to-all(bf16[32,32,2,12,128]{4,1,3,2,0:T(8,128)(2,1)S(1)} %copy_select_fusion), channel_id=1, replica_groups=mesh['dp'=8,'own'=32] {'own'}, dimensions={0} | all-to-all | bytes 12582912 | tf_op jit(solution)/shard_map/all_to_all | solution.py:165
  122.4 1.1 copy.101
  123.5 2.7 fusion.52
  126.2 4.5 %fusion = f32[32,128,128]{2,1,0:T(8,128)S(1)} fusion(bf16[32,1,384,128]{3,0,2,1:T(8,128)(2,1)S(1)} %get-tuple-element.29, bf16[32,128,768]{2,1,0:T(8,128)(2,1)} %all-gather.3.cloned.1.call-done), kind=kOutput, calls=%fused_computation.7 | convolution fusion | flops 402653184 | bytes 8388608 | tf_op jit(solution)/shard_map/kcs,ksw->kcw/dot_general | solution.py:169
  130.8 1.6 fusion.12
  132.5 2.0 copy.109
  134.5 11.4 %fusion.9 = bf16[32,384,128]{2,1,0:T(8,128)(2,1)} fusion(bf16[32,128,768]{2,1,0:T(8,128)(2,1)} %all-gather.3.cloned.1.call-done, f32[32,128,128]{2,1,0:T(8,128)} %copy-done.4, bf16[32,1,384,128]{3,0,2,1:T(8,128)(2,1)} %get-tuple-element.30), kind=kOutput, calls=%fused_computation.18 | convolution fusion | flops 816840704 | bytes 14680064 | tf_op jit(solution)/shard_map/kcs,kcw->ksw/dot_general | solution.py:177
  145.9 3.9 copy.107
  150.4 4.0 copy.110
  154.4 4.8 %all-to-all-start.1 = ((bf16[32,32,2,12,128]{4,1,3,2,0:T(8,128)(2,1)}), bf16[32,32,2,12,128]{4,1,3,2,0:T(8,128)(2,1)}, u32[]{:S(2)}, u32[]{:S(2)}) async-start(bf16[32,32,2,12,128]{4,1,3,2,0:T(8,128)(2,1)} %copy.110), calls=%async_computation.2 | async-start | bytes 12582912 | tf_op jit(solution)/shard_map/all_to_all | solution.py:183
  159.4 77.7 %all-to-all-done.1 = bf16[32,32,2,12,128]{4,1,3,2,0:T(8,128)(2,1)} async-done(((bf16[32,32,2,12,128]{4,1,3,2,0:T(8,128)(2,1)}), bf16[32,32,2,12,128]{4,1,3,2,0:T(8,128)(2,1)}, u32[]{:S(2)}, u32[]{:S(2)}) %all-to-all-start.1) | async-done | bytes 6291488 | tf_op jit(solution)/shard_map/all_to_all | solution.py:183
  237.1 9.0 %copy.111 = bf16[32,32,2,12,128]{4,3,2,1,0:T(8,128)(2,1)} copy(bf16[32,32,2,12,128]{4,1,3,2,0:T(8,128)(2,1)} %all-to-all-done.1) | data formatting | bytes 12582912 | tf_op jit(solution)/shard_map/all_to_all | solution.py:183
  246.1 12.2 %reshape.134 = bf16[1024,3072]{1,0:T(8,128)(2,1)} reshape(bf16[32,32,2,12,128]{4,3,2,1,0:T(8,128)(2,1)} %copy.111) | data formatting | bytes 12582912 | tf_op jit(solution)/shard_map/reshape | solution.py:128
  258.4 8.7 %copy.112 = bf16[3072,1024]{1,0:T(8,128)(2,1)} copy(bf16[3072,1024]{0,1:T(8,128)(2,1)} %bitcast.53) | data formatting | bytes 12582912 | tf_op jit(solution)/shard_map/dot_general | solution.py:129
  267.1 7.1 %subtract_convert_fusion = (bf16[64,2,12,128]{3,0,2,1:T(8,128)(2,1)}, f32[64,2,12,128]{3,0,2,1:T(8,128)}, f32[64,2,12,128]{3,0,2,1:T(8,128)}) fusion(bf16[64,2,12,128]{3,1,2,0:T(2,128)(2,1)S(1)} %constant_dynamic-slice_fusion, f32[64,2,12,128]{3,1,2,0:T(2,128)} %param.14, f32[64,2,12,128]{3,1,2,0:T(2,128)} %param.15, ...), kind=kOutput, calls=%fused_computation.38 | convolution fusion | flops 405471232 | bytes 10227712 | tf_op jit(solution)/shard_map/dot_general | solution.py:129
  274.3 7.5 %fusion.2 = f32[32,128,384]{2,1,0:T(8,128)} fusion(bf16[32,1,384,128]{3,0,2,1:T(8,128)(2,1)S(1)} %copy-done.2, f32[32,128,128]{2,1,0:T(8,128)} %copy-done.4), kind=kOutput, calls=%fused_computation.11 | convolution fusion | flops 407371776 | bytes 11534336 | tf_op jit(solution)/shard_map/kcw,ksw->kcs/dot_general | solution.py:172
  281.8 1.1 copy-done.3
  282.9 1.5 copy.115
  284.4 2.8 copy.116
  287.1 46.7 %all-gather.5.cloned.1.call-done = bf16[64,2,12,1024]{3,0,2,1:T(8,128)(2,1)} async-done(((bf16[64,2,12,128]{3,0,2,1:T(8,128)(2,1)}), bf16[64,2,12,1024]{3,0,2,1:T(8,128)(2,1)}) %all-gather.5.cloned.1.call-update) | async-done | bytes 3145744 | tf_op jit(solution)/shard_map/all_gather | solution.py:189
  333.8 6.8 %copy.114 = bf16[64,2,12,1024]{3,1,2,0:T(2,128)(2,1)} copy(bf16[64,2,12,1024]{3,0,2,1:T(8,128)(2,1)} %all-gather.5.cloned.1.call-done) | data formatting | bytes 6291456
  340.6 72.5 %reduce-scatter.2.cloned.1.call-done = f32[4,128,384]{2,1,0:T(8,128)} async-done(((f32[32,128,384]{2,1,0:T(8,128)}), f32[4,128,384]{2,1,0:T(8,128)}) %reduce-scatter.2.cloned.1.call-update) | async-done | bytes 786448 | tf_op jit(solution)/shard_map/reduce_scatter | solution.py:179
  413.1 1.2 convert_element_type.25
  414.3 1.8 gather_fusion.1
  (42 shorter events, 2.5 us)
Async XLA Ops:
  7.2 9.0 %copy-start = (bf16[64,2,12,1024]{3,1,2,0:T(2,128)(2,1)S(1)}, bf16[64,2,12,1024]{3,1,2,0:T(2,128)(2,1)}, u32[]{:S(2)}) copy-start(bf16[64,2,12,1024]{3,1,2,0:T(2,128)(2,1)} %param.13) | copy-start | bytes 9437188
  7.2 119.1 %all-gather.3.cloned.1.call-start = ((), (), s32[]{:S(2)}) async-start(), calls=%async_computation.3 | async-start | bytes 7077888 | tf_op jit(solution)/shard_map/all_gather | solution.py:157
  15.5 0.7 copy-start.5
  126.2 4.6 %copy-start.7 = (bf16[32,128,768]{2,1,0:T(8,128)(2,1)S(1)}, bf16[32,128,768]{2,1,0:T(8,128)(2,1)}, u32[]{:S(2)}) copy-start(bf16[32,128,768]{2,1,0:T(8,128)(2,1)} %all-gather.3.cloned.1.call-done) | copy-start | bytes 18874372
  130.8 1.6 copy-start.4
  154.4 4.9 %copy-start.6 = (s32[32,8,4]{2,1,0:T(8,128)S(1)}, s32[32,8,4]{2,1,0:T(8,128)}, u32[]{:S(2)}) copy-start(s32[32,8,4]{2,1,0:T(8,128)} %copy-done.5) | copy-start | bytes 12292
  154.4 82.7 %all-to-all-start.1 = ((bf16[32,32,2,12,128]{4,1,3,2,0:T(8,128)(2,1)}), bf16[32,32,2,12,128]{4,1,3,2,0:T(8,128)(2,1)}, u32[]{:S(2)}, u32[]{:S(2)}) async-start(bf16[32,32,2,12,128]{4,1,3,2,0:T(8,128)(2,1)} %copy.110), calls=%async_computation.2 | async-start | bytes 12582912 | tf_op jit(solution)/shard_map/all_to_all | solution.py:183
  159.3 174.5 %all-gather.5.cloned.1.call-start = ((), (), s32[]{:S(2)}) async-start(), calls=%async_computation.5 | async-start | bytes 3538944 | tf_op jit(solution)/shard_map/all_gather | solution.py:189
  267.1 7.2 %copy-start.2 = (bf16[32,1,384,128]{3,0,2,1:T(8,128)(2,1)S(1)}, bf16[32,1,384,128]{3,0,2,1:T(8,128)(2,1)}, u32[]{:S(2)}) copy-start(bf16[32,1,384,128]{3,0,2,1:T(8,128)(2,1)} %get-tuple-element.30) | copy-start | bytes 9437188
  274.2 138.9 %reduce-scatter.2.cloned.1.call-start = ((), (), s32[]{:S(2)}) async-start(), calls=%async_computation.4 | async-start | bytes 7077888 | tf_op jit(solution)/shard_map/reduce_scatter | solution.py:179
  281.7 1.1 copy-start.3
  284.4 131.8 %copy-start.1 = (bf16[64,2,12,1024]{3,1,2,0:T(2,128)(2,1)S(1)}, bf16[64,2,12,1024]{3,1,2,0:T(2,128)(2,1)}, u32[]{:S(2)}) copy-start(bf16[64,2,12,1024]{3,1,2,0:T(2,128)(2,1)} %param.13) | copy-start | bytes 9437188
Sparse Core Ops, SparseCore 0:
  14.6 78.3 all-gather.2
  274.3 59.4 all-gather.4
  336.4 76.7 reduce-scatter.1

commit v5 on v4

--- a/solution.py
+++ b/solution.py
@@ -176,11 +176,13 @@
     back_pre = (back_hidden * slopes).astype(jnp.bfloat16)
     grad_in = jnp.einsum("kcs,kcw->ksw", sig_slots, back_pre, preferred_element_type=jnp.float32)
     grad_out = jnp.einsum("kcs,kcw->ksw", cot_slots, hidden, preferred_element_type=jnp.float32)
+    grads = jnp.stack([grad_in, grad_out], axis=1).astype(jnp.bfloat16)
+    pred_part, grads = lax.optimization_barrier((pred_part, grads))
     pred_slots = lax.psum_scatter(pred_part, "dp", scatter_dimension=0, tiled=True)
-    pred_slots = pred_slots.astype(jnp.bfloat16)
-    grads = jnp.stack([grad_in, grad_out], axis=1).astype(jnp.bfloat16)
     pieces = grads.reshape(pairs, 2, n_own, piece_rows, width_part).transpose(2, 0, 1, 3, 4)
     arrived_grad = lax.all_to_all(pieces, "own", split_axis=0, concat_axis=0, tiled=True)
+    arrived_grad, pred_slots = lax.optimization_barrier((arrived_grad, pred_slots))
+    pred_slots = pred_slots.astype(jnp.bfloat16)
     table = sum_by_insertion(peer_rows, arrived_grad, number).reshape(
         number, 2, piece_rows, width_part
     )

time: 428 us -> 373 us (0.87)
  the two profiles are of different devices: /device:TPU:1 before, /device:TPU:32 now
where the time goes in v5:
time: 373 us; the launch traced here: 367 us
  waiting for transfers between devices  136 us (36%)
  local copies, waits for them, and re-layouts  80.6 us (22%)
  blocking collectives  80.1 us (21%)
  matrix products  33.6 us (9%)
  other arithmetic  17.7 us (5%)
  between operations  14.1 us (4%)
  starting transfers between devices  5.38 us (1%)
    all_to_all x1, blocking collectives, shards(): lax.all_to_all(outgoing, 'own', split_axis=0, concat_axis=0, tiled=True)  80.1 us
    all_to_all x1, waiting for transfers between devices, shards(): lax.all_to_all(pieces, 'own', split_axis=0, concat_axis=0, tiled=True)  78.8 us
    all_gather x1, waiting for transfers between devices, shards(): new_weights = lax.all_gather(fresh_part, 'dp', axis=3, tiled=True)  56.8 us
    gather x1, local copies, waits for them, and re-layouts, shards(): jnp.take(my_width, peer_rows, axis=0)  20.6 us
    reshape x1, local copies, waits for them, and re-layouts, sum_by_insertion(): flat_grad = arrived_grad.reshape(item_rows.shape[0], -1)  12 us
    unnamed x17, local copies, waits for them, and re-layouts  11.5 us
    dot_general x1, matrix products, shards(): jnp.einsum('kcs,kcw->ksw', sig_slots, back_pre, preferred_element_type=jn...  10.5 us
    optimization_barrier x1, local copies, waits for them, and re-layouts, shards(): lax.optimization_barrier((arrived_grad, pred_slots))  9.04 us
  transfers between devices with their start and end apart: 4, of which 2 were waited for; matrix products, arithmetic and copies ran while one was open for 13% of the time, Pallas kernels for 0%

profile of v5, /device:TPU:32, one launch (start us, length us, event | category | flops | bytes accessed | tf_op | source)
XLA Modules:
  0.0 367.2 jit_solution(746524388294055679)
XLA Ops:
  7.2 1.0 dynamic-slice_reduce_fusion
  8.3 0.8 compare_convert_fusion
  9.0 1.2 reduce-window.6
  10.6 0.8 fusion.40
  11.4 3.1 scatter_custom_fusion
  14.5 0.8 select_reduce_fusion
  15.8 0.4 copy-done.3
  16.6 20.6 %gather_fusion = bf16[1024,2,12,128]{3,1,2,0:T(2,128)(2,1)} fusion(bf16[64,2,12,128]{3,1,2,0:T(2,128)(2,1)S(1)} %constant_dynamic-slice_fusion, s32[1024]{0:T(1024)S(1)} %broadcast_clamp_fusion), kind=kCustom, calls=%fused_computation | custom fusion | bytes 12587008 | tf_op jit(solution)/shard_map/jit(_take)/gather | solution.py:162
  37.1 3.7 %copy_select_fusion = bf16[32,32,2,12,128]{4,1,3,2,0:T(8,128)(2,1)S(1)} fusion(bf16[32,32,2,12,128]{4,2,3,1,0:T(2,128)(2,1)} %bitcast.54, pred[32,32]{1,0:T(8,128)(4,1)S(1)} %copy.93), kind=kLoop, calls=%fused_computation.4 | loop fusion | flops 3145728 | bytes 12583936 | tf_op jit(solution)/shard_map/jit(_take)/select_n | solution.py:162
  40.9 80.1 %all_to_all.10 = bf16[32,32,2,12,128]{4,1,3,2,0:T(8,128)(2,1)S(1)} all-to-all(bf16[32,32,2,12,128]{4,1,3,2,0:T(8,128)(2,1)S(1)} %copy_select_fusion), channel_id=1, replica_groups=mesh['dp'=8,'own'=32] {'own'}, dimensions={0} | all-to-all | bytes 12582912 | tf_op jit(solution)/shard_map/all_to_all | solution.py:165
  121.0 1.1 copy.98
  122.1 2.7 fusion.49
  124.8 5.3 %fusion = f32[32,128,128]{2,1,0:T(8,128)S(1)} fusion(bf16[32,1,384,128]{3,0,2,1:T(8,128)(2,1)} %get-tuple-element.37, bf16[32,128,768]{2,1,0:T(8,128)(2,1)} %all-gather.3.cloned.1.call-done), kind=kOutput, calls=%fused_computation.7 | convolution fusion | flops 402653184 | bytes 8388608 | tf_op jit(solution)/shard_map/kcs,ksw->kcw/dot_general | solution.py:169
  130.1 1.3 copy-done.2
  131.4 6.0 %fusion.2 = f32[32,128,384]{2,1,0:T(8,128)} fusion(bf16[32,1,384,128]{3,0,2,1:T(8,128)(2,1)S(1)} %get-tuple-element.38, f32[32,128,128]{2,1,0:T(8,128)S(1)} %fusion), kind=kOutput, calls=%fused_computation.13 | convolution fusion | flops 407371776 | bytes 11534336 | tf_op jit(solution)/shard_map/kcw,ksw->kcs/dot_general | solution.py:172
  137.4 5.7 %convert_bitcast_fusion = bf16[32,1,384,128]{3,2,0,1:T(8,128)(2,1)} fusion(bf16[32,128,768]{2,1,0:T(8,128)(2,1)} %all-gather.3.cloned.1.call-done, f32[32,128,128]{2,1,0:T(8,128)} %copy-done.2), kind=kOutput, calls=%fused_computation.8 | convolution fusion | flops 408944640 | bytes 8388608 | tf_op jit(solution)/shard_map/kcs,kcw->ksw/dot_general | solution.py:178
  143.2 10.5 %convert_bitcast_fusion.1 = bf16[32,1,384,128]{3,2,0,1:T(8,128)(2,1)} fusion(bf16[32,128,768]{2,1,0:T(8,128)(2,1)} %all-gather.3.cloned.1.call-done, f32[32,128,128]{2,1,0:T(8,128)} %copy-done.2, bf16[32,1,384,128]{3,0,2,1:T(8,128)(2,1)S(1)} %get-tuple-element.38), kind=kOutput, calls=%fused_computation.9 | convolution fusion | flops 816840704 | bytes 14680064 | tf_op jit(solution)/shard_map/kcs,kcw->ksw/dot_general | solution.py:177
  153.7 6.1 %pad_maximum_fusion = bf16[32,2,384,128]{3,2,0,1:T(8,128)(2,1)} fusion(bf16[32,1,384,128]{3,2,0,1:T(8,128)(2,1)} %convert_bitcast_fusion, bf16[32,1,384,128]{3,2,0,1:T(8,128)(2,1)} %convert_bitcast_fusion.1), kind=kLoop, calls=%fused_computation.3 | loop fusion | flops 3145728 | bytes 12582912 | tf_op jit(solution)/shard_map/stack | solution.py:179
  159.8 6.8 %copy.103 = bf16[32,2,384,128]{3,0,2,1:T(8,128)(2,1)S(1)} copy(bf16[32,2,384,128]{3,2,0,1:T(8,128)(2,1)} %pad_maximum_fusion) | data formatting | bytes 12582912 | tf_op jit(solution)/shard_map/optimization_barrier | solution.py:180
  166.6 3.9 %copy.104 = bf16[32,32,2,12,128]{4,1,3,2,0:T(8,128)(2,1)} copy(bf16[32,32,2,12,128]{4,1,3,0,2:T(8,128)(2,1)S(1)} %bitcast.57) | data formatting | bytes 12582912 | tf_op jit(solution)/shard_map/transpose | solution.py:182
  170.5 5.0 %all-to-all-start.1 = ((bf16[32,32,2,12,128]{4,1,3,2,0:T(8,128)(2,1)}), bf16[32,32,2,12,128]{4,1,3,2,0:T(8,128)(2,1)}, u32[]{:S(2)}, u32[]{:S(2)}) async-start(bf16[32,32,2,12,128]{4,1,3,2,0:T(8,128)(2,1)} %copy.104), calls=%async_computation.1 | async-start | bytes 12582912 | tf_op jit(solution)/shard_map/all_to_all | solution.py:183
  176.0 78.8 %all-to-all-done.1 = bf16[32,32,2,12,128]{4,1,3,2,0:T(8,128)(2,1)} async-done(((bf16[32,32,2,12,128]{4,1,3,2,0:T(8,128)(2,1)}), bf16[32,32,2,12,128]{4,1,3,2,0:T(8,128)(2,1)}, u32[]{:S(2)}, u32[]{:S(2)}) %all-to-all-start.1) | async-done | bytes 6291488 | tf_op jit(solution)/shard_map/all_to_all | solution.py:183
  254.8 9.0 %copy.107 = bf16[32,32,2,12,128]{4,3,2,1,0:T(8,128)(2,1)} copy(bf16[32,32,2,12,128]{4,1,3,2,0:T(8,128)(2,1)} %all-to-all-done.1) | data formatting | bytes 12582912 | tf_op jit(solution)/shard_map/optimization_barrier | solution.py:184
  263.8 12.0 %reshape.131 = bf16[1024,3072]{1,0:T(8,128)(2,1)} reshape(bf16[32,32,2,12,128]{4,3,2,1,0:T(8,128)(2,1)} %copy.107) | data formatting | bytes 12582912 | tf_op jit(solution)/shard_map/reshape | solution.py:128
  275.9 8.8 %copy.108 = bf16[3072,1024]{1,0:T(8,128)(2,1)} copy(bf16[3072,1024]{0,1:T(8,128)(2,1)} %bitcast.58) | data formatting | bytes 12582912 | tf_op jit(solution)/shard_map/dot_general | solution.py:129
  284.7 6.1 %subtract_convert_fusion = (bf16[64,2,12,128]{3,0,2,1:T(8,128)(2,1)}, f32[64,2,12,128]{3,0,2,1:T(8,128)S(1)}, f32[64,2,12,128]{3,0,2,1:T(8,128)S(1)}) fusion(bf16[64,2,12,128]{3,1,2,0:T(2,128)(2,1)S(1)} %constant_dynamic-slice_fusion, f32[64,2,12,128]{3,1,2,0:T(2,128)S(1)} %copy-done.5, f32[64,2,12,128]{3,1,2,0:T(2,128)S(1)} %copy-done.6, ...), kind=kOutput, calls=%fused_computation.38 | convolution fusion | flops 405471232 | bytes 10227712 | tf_op jit(solution)/shard_map/dot_general | solution.py:129
  290.8 1.2 convert_element_type.25
  292.0 1.5 copy.111
  293.5 1.5 copy.112
  295.0 1.8 gather_fusion.1
  296.8 56.8 %all-gather.5.cloned.1.call-done = bf16[64,2,12,1024]{3,0,2,1:T(8,128)(2,1)} async-done(((bf16[64,2,12,128]{3,0,2,1:T(8,128)(2,1)}), bf16[64,2,12,1024]{3,0,2,1:T(8,128)(2,1)}) %all-gather.5.cloned.1.call-update) | async-done | bytes 3145744 | tf_op jit(solution)/shard_map/all_gather | solution.py:191
  353.6 6.8 %copy.110 = bf16[64,2,12,1024]{3,1,2,0:T(2,128)(2,1)} copy(bf16[64,2,12,1024]{3,0,2,1:T(8,128)(2,1)} %all-gather.5.cloned.1.call-done) | data formatting | bytes 6291456
  (39 shorter events, 1.7 us)
Async XLA Ops:
  7.2 9.1 %copy-start = (bf16[64,2,12,1024]{3,1,2,0:T(2,128)(2,1)S(1)}, bf16[64,2,12,1024]{3,1,2,0:T(2,128)(2,1)}, u32[]{:S(2)}) copy-start(bf16[64,2,12,1024]{3,1,2,0:T(2,128)(2,1)} %param.13) | copy-start | bytes 9437188
  7.2 117.6 %all-gather.3.cloned.1.call-start = ((), (), s32[]{:S(2)}) async-start(), calls=%async_computation.3 | async-start | bytes 7077888 | tf_op jit(solution)/shard_map/all_gather | solution.py:157
  14.5 240.3 %reduce-scatter.2.cloned.1.call-start = ((), (), s32[]{:S(2)}) async-start(), calls=%async_computation.4 | async-start | bytes 7077888 | tf_op jit(solution)/shard_map/reduce_scatter | solution.py:181
  15.6 0.7 copy-start.3
  130.1 1.3 copy-start.2
  170.5 5.3 %copy-start.4 = (s32[32,8,4]{2,1,0:T(8,128)S(1)}, s32[32,8,4]{2,1,0:T(8,128)}, u32[]{:S(2)}) copy-start(s32[32,8,4]{2,1,0:T(8,128)} %copy-done.3) | copy-start | bytes 12292
  170.5 84.3 %all-to-all-start.1 = ((bf16[32,32,2,12,128]{4,1,3,2,0:T(8,128)(2,1)}), bf16[32,32,2,12,128]{4,1,3,2,0:T(8,128)(2,1)}, u32[]{:S(2)}, u32[]{:S(2)}) async-start(bf16[32,32,2,12,128]{4,1,3,2,0:T(8,128)(2,1)} %copy.104), calls=%async_computation.1 | async-start | bytes 12582912 | tf_op jit(solution)/shard_map/all_to_all | solution.py:183
  175.6 178.1 %all-gather.5.cloned.1.call-start = ((), (), s32[]{:S(2)}) async-start(), calls=%async_computation.5 | async-start | bytes 3538944 | tf_op jit(solution)/shard_map/all_gather | solution.py:191
  275.9 8.8 %copy-start.5 = (f32[64,2,12,128]{3,1,2,0:T(2,128)S(1)}, f32[64,2,12,128]{3,1,2,0:T(2,128)}, u32[]{:S(2)}) copy-start(f32[64,2,12,128]{3,1,2,0:T(2,128)} %param.14) | copy-start | bytes 2359300
  275.9 8.8 %copy-start.6 = (f32[64,2,12,128]{3,1,2,0:T(2,128)S(1)}, f32[64,2,12,128]{3,1,2,0:T(2,128)}, u32[]{:S(2)}) copy-start(f32[64,2,12,128]{3,1,2,0:T(2,128)} %param.15) | copy-start | bytes 2359300
  295.0 65.5 %copy-start.1 = (bf16[64,2,12,1024]{3,1,2,0:T(2,128)(2,1)S(1)}, bf16[64,2,12,1024]{3,1,2,0:T(2,128)(2,1)}, u32[]{:S(2)}) copy-start(bf16[64,2,12,1024]{3,1,2,0:T(2,128)(2,1)} %param.13) | copy-start | bytes 9437188
Sparse Core Ops, SparseCore 0:
  14.6 75.2 all-gather.2
  159.9 72.6 reduce-scatter.1
  290.9 62.6 all-gather.4
